TPU v7x, 256 devices: a whole 4x4x8 slice. The times are simulated.
256 devices in a mesh: group: 16 (over z, core), shard: 16 (over y, x).
Axes of the slice: x: 4, y: 4, z: 8, core: 2. Of those that a mesh axis runs over, the one named last changes fastest.
Arguments:
- tokens: bfloat16 [512, 1280], P(('group', 'shard')), as said below
- kv_cache: bfloat16 [512, 128, 2560], P(('group', 'shard'))
- keep_list: int32 [512, 128], P(('group', 'shard')), may hold values from 0 to 1
- lengths: int32 [512], P(('group', 'shard')), may hold values from 64 to 128
- merge_index: int32 [512, 128], P(('group', 'shard')), may hold values from 0 to 15
- merge_table: bfloat16 [16], replicated, may hold values from 0.0099487305 to 0.099609375
- move_offset: int32 [16, 2], P('shard'), may hold values from 0 to 15, as said below
- pair_mask: int32 [16], P('shard'), may hold values from 1 to 15
- w_qkv: bfloat16 [1280, 3840], P(None, 'shard'), may hold values from -0.15625 to 0.15625
- w_out: bfloat16 [1280, 1280], P(None, 'shard'), may hold values from -0.15625 to 0.15625
- w_up: bfloat16 [1280, 5120], P(None, 'shard'), may hold values from -0.15625 to 0.15625
- w_gate: bfloat16 [1280, 5120], P(None, 'shard'), may hold values from -0.15625 to 0.15625
- w_down: bfloat16 [5120, 1280], P('shard'), may hold values from -0.078125 to 0.078125
- qk_scale: float32 [1280], replicated, may hold values from 0.5 to 2
- attn_rate: float32 [1280], replicated, may hold values from 0.05 to 0.5
- mlp_rate: float32 [1280], replicated, may hold values from 0.05 to 0.5
- up_scale: float32 [5120], P('shard'), may hold values from 0.5 to 2
- gate_scale: float32 [5120], P('shard'), may hold values from 0.5 to 2
Outputs:
- new_hidden: bfloat16 [512, 1280], P(('group', 'shard'))
- moved_cache: bfloat16 [512, 128, 2560], P(('group', 'shard'))
Inputs may be any that keep to these rules, and one draw needn't show every extreme that they name: `tokens`: slot 1 of group g and shard s holds the same token as that slot of group g XOR pair_mask[s] on shard s. `move_offset`: the 2 offsets of one shard index are distinct.
All inputs are finite; a program needn't handle non-finite values.
Results may differ from a plain program's by a relative error of at most 0.011.
Values may be sent and summed in bfloat16 or wider, within the bound.
A program may use at most 128 MiB of HBM per device.

v0:
```python
import jax
import jax.numpy as jnp
from jax import lax
from jax.sharding import PartitionSpec as P

DH = 64
BLOCK = 128
WTAB = 16


EPSILON = 1e-06
NEGATIVE = -1e30


def rms_normal(vector):
    return vector * lax.rsqrt(jnp.mean(vector * vector, axis=-1, keepdims=True) + EPSILON)


def head_normal(vector, scaling):
    return vector * lax.rsqrt(jnp.sum(vector * vector, axis=-1, keepdims=True) + EPSILON) * scaling


def rounded(vector):
    return lax.optimization_barrier(vector.astype(jnp.bfloat16)).astype(jnp.float32)


def spread_columns(row_block, weight):
    columns = jnp.dot(
        lax.all_gather(row_block, "shard", axis=0, tiled=True),
        weight,
        preferred_element_type=jnp.float32,
    ).astype(jnp.bfloat16)
    return lax.all_to_all(columns, "shard", split_axis=0, concat_axis=1, tiled=True)


def compact_local(kv_cache, keep_list, lengths, merge_index, merge_table):
    slot_count, context, doubled = kv_cache.shape
    block_count = context // BLOCK
    in_length = jnp.arange(context, dtype=jnp.int32)[None, :] < lengths[:, None]
    keeper = (keep_list == 1) & in_length
    dropper = (keep_list == 0) & in_length
    position = jnp.cumsum(keeper.astype(jnp.int32), axis=1) - 1
    kept_count = jnp.sum(keeper.astype(jnp.int32), axis=1)
    drop_count = jnp.sum(dropper.astype(jnp.int32), axis=1)
    table_hits = merge_index[:, :, None] == jnp.arange(WTAB, dtype=jnp.int32)[None, None, :]
    weights = jnp.sum(
        jnp.where(table_hits, merge_table.astype(jnp.float32)[None, None, :], 0.0), axis=2
    ) * dropper.astype(jnp.float32)
    target = jnp.arange(BLOCK, dtype=jnp.int32)
    placing = (position[:, None, :] == target[None, :, None]) & keeper[:, None, :]
    summing = jnp.where(
        target[None, :, None] == kept_count[:, None, None], weights[:, None, :], 0.0
    )
    mixing = (placing.astype(jnp.float32) + summing).astype(jnp.bfloat16)
    packed = jnp.einsum(
        "ndk,nkc->ndc", mixing, kv_cache, preferred_element_type=jnp.float32
    ).astype(jnp.bfloat16)
    live_count = (kept_count + (drop_count > 0).astype(jnp.int32)).reshape(slot_count, block_count)
    return (packed, live_count.astype(jnp.bfloat16))


def per_device(
    tokens,
    kv_cache,
    keep_list,
    lengths,
    merge_index,
    merge_table,
    move_offset,
    pair_mask,
    w_qkv,
    w_out,
    w_up,
    w_gate,
    w_down,
    qk_scale,
    attn_rate,
    mlp_rate,
    up_scale,
    gate_scale,
):
    slot_count, context, doubled = kv_cache.shape
    model_width = tokens.shape[1]
    head_count = model_width // DH
    group_count = lax.axis_size("group")
    group_index = lax.axis_index("group")
    packed, live_count = compact_local(kv_cache, keep_list, lengths, merge_index, merge_table)
    offsets = move_offset[0]
    target = (group_index + offsets) % group_count
    sender = (jnp.arange(group_count, dtype=jnp.int32)[:, None] == target[None, :]).astype(
        jnp.bfloat16
    )
    outgoing = jnp.einsum("pj,jrc->prc", sender, packed, preferred_element_type=jnp.float32).astype(
        jnp.bfloat16
    )
    outgoing_live = jnp.einsum(
        "pj,jb->pb", sender, live_count, preferred_element_type=jnp.float32
    ).astype(jnp.bfloat16)
    incoming, incoming_live = (
        lax.all_to_all(outgoing, "group", split_axis=0, concat_axis=0, tiled=True),
        lax.all_to_all(outgoing_live, "group", split_axis=0, concat_axis=0, tiled=True),
    )
    source = (group_index - offsets) % group_count
    picker = (source[:, None] == jnp.arange(group_count, dtype=jnp.int32)[None, :]).astype(
        jnp.bfloat16
    )
    moved_cache = jnp.einsum(
        "jp,prc->jrc", picker, incoming, preferred_element_type=jnp.float32
    ).astype(jnp.bfloat16)
    moved_live = jnp.einsum("jp,pb->jb", picker, incoming_live, preferred_element_type=jnp.float32)
    projected = spread_columns(tokens, w_qkv)
    head_scale = qk_scale.reshape(head_count, DH)
    queries = head_normal(
        projected[:, :model_width].astype(jnp.float32).reshape(slot_count, head_count, DH),
        head_scale,
    ).astype(jnp.bfloat16)
    new_keys = head_normal(
        projected[:, model_width : 2 * model_width]
        .astype(jnp.float32)
        .reshape(slot_count, head_count, DH),
        head_scale,
    ).astype(jnp.bfloat16)
    new_values = projected[:, 2 * model_width :].reshape(slot_count, head_count, DH)
    key_rows = moved_cache[:, :, :model_width].reshape(slot_count, context, head_count, DH)
    value_rows = moved_cache[:, :, model_width:].reshape(slot_count, context, head_count, DH)
    score_scale = float(DH) ** 0.5
    scores = score_scale * jnp.einsum(
        "jhd,jrhd->jhr", queries, key_rows, preferred_element_type=jnp.float32
    )
    fresh_score = score_scale * jnp.sum(
        queries.astype(jnp.float32) * new_keys.astype(jnp.float32), axis=-1
    )
    row_valid = (jnp.arange(context, dtype=jnp.int32) % BLOCK).astype(jnp.float32)[
        None, :
    ] < jnp.repeat(moved_live, BLOCK, axis=1)
    pair_bits = pair_mask[0]
    partner = jnp.bitwise_xor(group_index, pair_bits)
    with_new = (jnp.arange(slot_count, dtype=jnp.int32) < slot_count - 1) | (group_index < partner)
    highest = jnp.maximum(
        jnp.max(jnp.where(row_valid[:, None, :], scores, NEGATIVE), axis=2),
        jnp.where(with_new[:, None], fresh_score, NEGATIVE),
    )
    safe_scores = jnp.where(row_valid[:, None, :], scores, highest[:, :, None])
    soft_weights = jnp.where(row_valid[:, None, :], jnp.exp(safe_scores - highest[:, :, None]), 0.0)
    fresh_weight = jnp.where(with_new[:, None], jnp.exp(fresh_score - highest), 0.0)
    weight_sum = jnp.sum(soft_weights, axis=2) + fresh_weight
    weighted = jnp.einsum(
        "jhr,jrhd->jhd",
        soft_weights.astype(jnp.bfloat16),
        value_rows,
        preferred_element_type=jnp.float32,
    )
    weighted = weighted + rounded(fresh_weight)[:, :, None] * new_values.astype(jnp.float32)
    last_high = highest[slot_count - 1 :]
    last_sum = weight_sum[slot_count - 1 :]
    last_weighted = weighted[slot_count - 1 :]
    gathered_high, gathered_sum, gathered_weighted = (
        lax.all_gather(last_high, "group", axis=0, tiled=True),
        lax.all_gather(last_sum, "group", axis=0, tiled=True),
        lax.all_gather(last_weighted, "group", axis=0, tiled=True),
    )
    picker_group = (jnp.arange(group_count, dtype=jnp.int32) == partner).astype(jnp.float32)
    other_high = jnp.sum(picker_group[:, None] * gathered_high, axis=0, keepdims=True)
    other_sum = jnp.sum(picker_group[:, None] * gathered_sum, axis=0, keepdims=True)
    other_weighted = jnp.sum(picker_group[:, None, None] * gathered_weighted, axis=0, keepdims=True)
    merged = jnp.maximum(last_high, other_high)
    own_factor = jnp.exp(last_high - merged)
    other_factor = jnp.exp(other_high - merged)
    long_sum = last_sum * own_factor + other_sum * other_factor
    long_weighted = (
        last_weighted * own_factor[:, :, None] + other_weighted * other_factor[:, :, None]
    )
    weight_sum = jnp.concatenate([weight_sum[: slot_count - 1], long_sum], axis=0)
    weighted = jnp.concatenate([weighted[: slot_count - 1], long_weighted], axis=0)
    attended = (
        (weighted / weight_sum[:, :, None]).reshape(slot_count, model_width).astype(jnp.bfloat16)
    )
    attention_out = spread_columns(attended, w_out)
    hidden = tokens.astype(jnp.float32)
    mixed = rms_normal(
        hidden + attn_rate * (rms_normal(attention_out.astype(jnp.float32)) - hidden)
    )
    mixed_low = mixed.astype(jnp.bfloat16)
    gate_factor = gate_scale * float(model_width) ** 0.5
    shard_rows = lax.all_gather(mixed_low, "shard", axis=0, tiled=True)
    up_part = jnp.dot(shard_rows, w_up, preferred_element_type=jnp.float32) * up_scale
    gate_part = jnp.dot(shard_rows, w_gate, preferred_element_type=jnp.float32) * gate_factor
    inner = (up_part * jax.nn.silu(gate_part)).astype(jnp.bfloat16)
    partial_terms = jnp.dot(inner, w_down, preferred_element_type=jnp.float32)
    mlp_out = lax.psum_scatter(
        partial_terms.astype(jnp.bfloat16), "shard", scatter_dimension=0, tiled=True
    ).astype(jnp.float32)
    new_hidden = rms_normal(mixed + mlp_rate * (rms_normal(mlp_out) - mixed)).astype(jnp.bfloat16)
    return (new_hidden, moved_cache)


def solution(mesh):
    return jax.shard_map(
        per_device,
        mesh=mesh,
        in_specs=(
            P(("group", "shard"), None),
            P(("group", "shard"), None, None),
            P(("group", "shard"), None),
            P(("group", "shard")),
            P(("group", "shard"), None),
            P(),
            P("shard", None),
            P("shard"),
            P(None, "shard"),
            P(None, "shard"),
            P(None, "shard"),
            P(None, "shard"),
            P("shard", None),
            P(),
            P(),
            P(),
            P("shard"),
            P("shard"),
        ),
        out_specs=(P(("group", "shard"), None), P(("group", "shard"), None, None)),
        check_vma=False,
    )
```

profile of v0, /device:TPU:1, one launch (start us, length us, event | category | flops | bytes accessed | tf_op | source)
XLA Modules:
  0.0 548.7 jit_solution(16223864282160331246)
XLA Ops:
  7.2 0.8 convert_element_type.140
  7.9 0.8 select_reduce_fusion.1
  8.7 0.8 fusion.64
  9.5 0.8 broadcast_select_fusion
  10.2 0.7 fusion.43
  10.9 0.1 convert_reduce_fusion
  11.1 0.2 fusion.9
  11.2 0.7 copy.91
  11.9 10.0 %all-to-all-start = ((bf16[16,1,1]{2,1,0:T(2,128)(2,1)}), bf16[16,1,1]{2,1,0:T(2,128)(2,1)S(1)}, u32[]{:S(2)}, u32[]{:S(2)}) async-start(bf16[16,1,1]{2,1,0:T(2,128)(2,1)} %copy.91), calls=%async_computation | async-start | bytes 16384 | tf_op jit(solution)/shard_map/all_to_all | solution.py:101
  22.0 0.3 reduce_window_sum.11
  22.3 18.7 %all-gather = bf16[16,2,1280]{2,1,0:T(2,128)(2,1)S(1)} all-gather(bf16[1,2,1280]{2,1,0:T(2,128)(2,1)} %bitcast.99), channel_id=1, replica_groups=mesh['group'=16,'shard'=16] {'shard'}, dimensions={0}, use_global_device_ids=true | all-gather | bytes 87040 | tf_op jit(solution)/shard_map/all_gather | solution.py:29
  41.1 1.3 convolution_convert_fusion.3
  42.4 0.6 convolution_convert_fusion.1
  43.0 0.6 all_to_all.35
  43.7 4.7 all-to-all-start.1
  48.4 6.1 %convolution_convert_fusion = bf16[16,128,2560]{2,0,1:T(8,128)(2,1)} fusion(bf16[2,128,2560]{2,1,0:T(8,128)(2,1)S(1)} %convolution_convert_fusion.1, s32[2]{0:T(128)S(1)} %fusion.43), kind=kOutput, calls=%fused_computation.2 | convolution fusion | flops 26214432 | bytes 11796488 | tf_op jit(solution)/shard_map/pj,jrc->prc/dot_general | solution.py:93
  54.4 13.7 %copy.94 = bf16[16,128,2560]{2,1,0:T(8,128)(2,1)} copy(bf16[16,128,2560]{2,0,1:T(8,128)(2,1)} %convolution_convert_fusion) | data formatting | bytes 20971520 | tf_op jit(solution)/shard_map/convert_element_type | solution.py:93
  68.2 12.6 %all-to-all-start.2 = ((bf16[16,128,2560]{2,1,0:T(8,128)(2,1)}), bf16[16,128,2560]{2,1,0:T(8,128)(2,1)}, u32[]{:S(2)}, u32[]{:S(2)}) async-start(bf16[16,128,2560]{2,1,0:T(8,128)(2,1)} %copy.94), calls=%async_computation.2 | async-start | bytes 20971520 | tf_op jit(solution)/shard_map/all_to_all | solution.py:100
  81.5 0.2 reduce.2
  81.7 0.2 convolution_bitcast_fusion
  82.0 0.1 all_to_all.38
  82.2 0.1 reshape.274
  82.2 0.1 reshape.272
  82.3 0.1 reshape.275
  82.4 0.1 multiply_reduce_fusion.2
  82.5 0.1 multiply_reduce_fusion.3
  82.6 0.2 multiply_reduce_fusion.1
  82.8 226.4 %all-to-all-done.2 = bf16[16,128,2560]{2,1,0:T(8,128)(2,1)} async-done(((bf16[16,128,2560]{2,1,0:T(8,128)(2,1)}), bf16[16,128,2560]{2,1,0:T(8,128)(2,1)}, u32[]{:S(2)}, u32[]{:S(2)}) %all-to-all-start.2) | async-done | bytes 10485792 | tf_op jit(solution)/shard_map/all_to_all | solution.py:100
  309.2 15.7 %fusion.2 = bf16[2,128,2560]{2,0,1:T(2,128)(2,1)S(1)} fusion(bf16[16,128,2560]{2,1,0:T(8,128)(2,1)} %all-to-all-done.2, s32[2]{0:T(128)S(1)} %and_select_fusion.1), kind=kOutput, calls=%fused_computation.3 | convolution fusion | flops 21626912 | bytes 11796488 | tf_op jit(solution)/shard_map/jp,prc->jrc/dot_general | solution.py:107
  324.9 1.7 fusion.65
  326.6 3.0 copy.96
  329.6 1.4 fusion.25
  330.9 0.1 select_reduce_fusion
  331.1 0.1 copy.97
  331.2 0.1 copy.98
  331.3 16.2 %all-gather.1 = f32[16,1,20]{2,1,0:T(1,128)S(1)} all-gather(f32[1,1,20]{2,1,0:T(1,128)S(1)} %slice_bitcast_fusion.1), channel_id=1, replica_groups=mesh['group'=16,'shard'=16] {'group'}, dimensions={0}, use_global_device_ids=true | all-gather | bytes 1360 | tf_op jit(solution)/shard_map/all_gather | solution.py:158
  347.6 0.1 convert_bitcast_fusion.1
  347.7 0.1 reduce_sum.137
  347.8 0.1 copy.100
  347.9 14.5 %all-gather.2 = f32[16,1,20]{2,1,0:T(1,128)S(1)} all-gather(f32[1,1,20]{2,1,0:T(1,128)S(1)} %slice_bitcast_fusion), channel_id=1, replica_groups=mesh['group'=16,'shard'=16] {'group'}, dimensions={0}, use_global_device_ids=true | all-gather | bytes 1360 | tf_op jit(solution)/shard_map/all_gather | solution.py:159
  362.3 0.1 multiply_reduce_fusion.7
  362.5 0.1 div.28
  362.6 1.9 copy.99
  364.5 1.5 fusion.23
  366.1 17.1 %all_gather.20 = f32[16,20,64]{2,1,0:T(8,128)S(1)} all-gather(f32[1,20,64]{2,1,0:T(8,128)S(1)} %slice.46), channel_id=1, replica_groups=mesh['group'=16,'shard'=16] {'group'}, dimensions={0}, use_global_device_ids=true | all-gather | bytes 87040 | tf_op jit(solution)/shard_map/all_gather | solution.py:160
  383.2 0.1 multiply_reduce_fusion
  383.6 20.5 %all-gather.3 = bf16[16,2,1280]{2,1,0:T(2,128)(2,1)} all-gather(bf16[1,2,1280]{2,1,0:T(2,128)(2,1)S(1)} %fusion.36), channel_id=1, replica_groups=mesh['group'=16,'shard'=16] {'shard'}, dimensions={0}, use_global_device_ids=true | all-gather | bytes 87040 | tf_op jit(solution)/shard_map/all_gather | solution.py:29
  404.1 0.9 reshape.284
  405.0 1.7 convolution_convert_fusion.4
  406.8 4.4 all-to-all-start.3
  411.3 6.3 %all-to-all-done.3 = bf16[16,2,80]{2,1,0:T(2,128)(2,1)S(1)} async-done(((bf16[16,2,80]{2,1,0:T(2,128)(2,1)}), bf16[16,2,80]{2,1,0:T(2,128)(2,1)S(1)}, u32[]{:S(2)}, u32[]{:S(2)}) %all-to-all-start.3) | async-done | bytes 5152 | tf_op jit(solution)/shard_map/all_to_all | solution.py:33
  417.5 0.1 reshape.276
  417.6 0.1 fusion.27
  417.8 0.2 multiply_reduce_fusion.5
  418.1 18.0 %all-gather.4 = bf16[16,2,1280]{2,1,0:T(2,128)(2,1)} all-gather(bf16[1,2,1280]{2,1,0:T(2,128)(2,1)S(1)} %fusion.35), channel_id=1, replica_groups=mesh['group'=16,'shard'=16] {'shard'}, dimensions={0}, use_global_device_ids=true | all-gather | bytes 87040 | tf_op jit(solution)/shard_map/all_gather | solution.py:185
  436.1 0.9 reshape.286
  437.0 2.1 convolution_multiply_fusion
  439.1 2.6 convolution_convert_fusion.2
  441.8 0.6 dynamic-slice
  443.0 1.2 copy.102
  444.2 95.2 %all-reduce.3.cloned.1.call-done = bf16[32,1280]{1,0:T(8,128)(2,1)} async-done(((bf16[32,1280]{1,0:T(8,128)(2,1)}), bf16[32,1280]{1,0:T(8,128)(2,1)}) %all-reduce.3.cloned.1.call-update) | async-done | bytes 81936
  539.4 0.9 fusion.30
  540.3 0.9 multiply_reduce_fusion.4
  541.2 0.7 multiply_convert_fusion.2
  (56 shorter events, 1.1 us)
Async XLA Ops:
  7.2 35.3 %copy-start = (bf16[2,128,2560]{2,1,0:T(8,128)(2,1)S(1)}, bf16[2,128,2560]{2,1,0:T(8,128)(2,1)}, u32[]{:S(2)}) copy-start(bf16[2,128,2560]{2,1,0:T(8,128)(2,1)} %param.19) | copy-start | bytes 3932164
  11.9 31.7 %all-to-all-start = ((bf16[16,1,1]{2,1,0:T(2,128)(2,1)}), bf16[16,1,1]{2,1,0:T(2,128)(2,1)S(1)}, u32[]{:S(2)}, u32[]{:S(2)}) async-start(bf16[16,1,1]{2,1,0:T(2,128)(2,1)} %copy.91), calls=%async_computation | async-start | bytes 16384 | tf_op jit(solution)/shard_map/all_to_all | solution.py:101
  43.7 24.5 %all-to-all-start.1 = ((bf16[16,2,240]{2,1,0:T(2,128)(2,1)}), bf16[16,2,240]{2,1,0:T(2,128)(2,1)S(1)}, u32[]{:S(2)}, u32[]{:S(2)}) async-start(bf16[16,2,240]{2,1,0:T(2,128)(2,1)} %all_to_all.35), calls=%async_computation.1 | async-start | bytes 32768 | tf_op jit(solution)/shard_map/all_to_all | solution.py:33
  68.2 12.6 %copy-start.4 = (f32[1280]{0:T(1024)S(1)}, f32[1280]{0:T(1024)}, u32[]{:S(2)}) copy-start(f32[1280]{0:T(1024)} %param.31) | copy-start | bytes 15364
  68.2 13.3 %copy-start.7 = (s32[1,2]{1,0:T(1,128)S(1)}, s32[1,2]{1,0:T(1,128)}, u32[]{:S(2)}) copy-start(s32[1,2]{1,0:T(1,128)} %param.24) | copy-start | bytes 28
  68.2 241.0 %all-to-all-start.2 = ((bf16[16,128,2560]{2,1,0:T(8,128)(2,1)}), bf16[16,128,2560]{2,1,0:T(8,128)(2,1)}, u32[]{:S(2)}, u32[]{:S(2)}) async-start(bf16[16,128,2560]{2,1,0:T(8,128)(2,1)} %copy.94), calls=%async_computation.2 | async-start | bytes 20971520 | tf_op jit(solution)/shard_map/all_to_all | solution.py:100
  362.6 48.6 %copy-start.6 = (f32[320]{0:T(512)S(1)}, f32[320]{0:T(512)}, u32[]{:S(2)}) copy-start(f32[320]{0:T(512)} %param.35) | copy-start | bytes 3844
  364.5 53.3 %copy-start.2 = (bf16[2,1280]{1,0:T(2,128)(2,1)S(1)}, bf16[2,1280]{1,0:T(2,128)(2,1)}, u32[]{:S(2)}) copy-start(bf16[2,1280]{1,0:T(2,128)(2,1)} %param.18) | copy-start | bytes 15364
  364.5 53.3 %copy-start.3 = (f32[1280]{0:T(1024)S(1)}, f32[1280]{0:T(1024)}, u32[]{:S(2)}) copy-start(f32[1280]{0:T(1024)} %param.32) | copy-start | bytes 15364
  366.1 73.1 %copy-start.1 = (bf16[320,1280]{1,0:T(8,128)(2,1)S(1)}, bf16[320,1280]{1,0:T(8,128)(2,1)}, u32[]{:S(2)}) copy-start(bf16[320,1280]{1,0:T(8,128)(2,1)} %param.30) | copy-start | bytes 2457604
  406.8 10.8 %all-to-all-start.3 = ((bf16[16,2,80]{2,1,0:T(2,128)(2,1)}), bf16[16,2,80]{2,1,0:T(2,128)(2,1)S(1)}, u32[]{:S(2)}, u32[]{:S(2)}) async-start(bf16[16,2,80]{2,1,0:T(2,128)(2,1)} %bitcast.27), calls=%async_computation.3 | async-start | bytes 16384 | tf_op jit(solution)/shard_map/all_to_all | solution.py:33
  411.2 128.2 %all-reduce.3.cloned.1.call-start = ((), (), s32[]{:S(2)}) async-start(), calls=%async_computation.4 | async-start | bytes 163840
  437.0 4.7 copy-start.8
  443.0 97.3 %copy-start.5 = (f32[1280]{0:T(1024)S(1)}, f32[1280]{0:T(1024)}, u32[]{:S(2)}) copy-start(f32[1280]{0:T(1024)} %param.33) | copy-start | bytes 15364
Sparse Core Ops, SparseCore 0:
  441.9 97.4 all-reduce.2
where the time goes:
time: 550 us; the launch traced here: 549 us
  waiting for transfers between devices  328 us (60%)
  blocking collectives  105 us (19%)
  matrix products  33.4 us (6%)
  starting transfers between devices  31.7 us (6%)
  local copies, waits for them, and re-layouts  26.5 us (5%)
  between operations  15.6 us (3%)
  other arithmetic  8.59 us (2%)
    all_to_all x1, waiting for transfers between devices, per_device(): lax.all_to_all(outgoing, 'group', split_axis=0, concat_axis=0, tiled=True)  226 us
    unnamed x2, waiting for transfers between devices  95.2 us
    all_gather x2, blocking collectives, spread_columns(): lax.all_gather(row_block, 'shard', axis=0, tiled=True)  39.3 us
    all_gather x1, blocking collectives, per_device(): shard_rows = lax.all_gather(mixed_low, 'shard', axis=0, tiled=True)  18 us
    all_gather x1, blocking collectives, per_device(): lax.all_gather(last_weighted, 'group', axis=0, tiled=True)  17.1 us
    all_gather x1, blocking collectives, per_device(): lax.all_gather(last_high, 'group', axis=0, tiled=True)  16.2 us
    dot_general x1, matrix products, per_device(): jnp.einsum('jp,prc->jrc', picker, incoming, preferred_element_type=jnp.fl...  15.7 us
    all_gather x1, blocking collectives, per_device(): lax.all_gather(last_sum, 'group', axis=0, tiled=True)  14.5 us
  transfers between devices with their start and end apart: 5, of which 3 were waited for; matrix products, arithmetic and copies ran while one was open for 5% of the time, Pallas kernels for 0%

commit v1 on v0

v1 whole, which is shorter than its diff:
```python
import functools
import math

import jax
import jax.numpy as jnp
from jax import lax
from jax.experimental import pallas as pl
from jax.experimental.pallas import tpu as pltpu
from jax.sharding import PartitionSpec as P

DH = 64
WTAB = 16
N = 16
D = 1280
HEADS_PAD = 32
EPSILON = 1e-06
NEGATIVE = -1e30
MESH = pl.DeviceIdType.MESH
F32 = jnp.float32
BF16 = jnp.bfloat16


def iota(shape, axis):
    return lax.broadcasted_iota(jnp.int32, shape, axis)


def rms_normal(vector):
    return vector * lax.rsqrt(jnp.mean(vector * vector, axis=-1, keepdims=True) + EPSILON)


def wait_for(ref, sem):
    pltpu.make_async_copy(ref, ref, sem).wait()


def layer_kernel(
    lengths,
    offsets,
    pair_bits,
    keep_ref,
    index_ref,
    table_ref,
    qk_ref,
    attn_rate_ref,
    mlp_rate_ref,
    up_scale_ref,
    gate_scale_ref,
    tokens_hbm,
    kv_hbm,
    w_qkv_hbm,
    w_out_hbm,
    w_up_hbm,
    w_gate_hbm,
    w_down_hbm,
    hidden_out,
    cache_out,
    kv,
    w_qkv,
    w_out,
    w_up,
    w_gate,
    w_down,
    packed,
    arrived,
    staged,
    group_rows,
    shard_rows,
    lhs,
    qkv_send,
    qkv_recv,
    qkv_flat,
    partial,
    attended_rows,
    out_send,
    out_recv,
    out_flat,
    mixed_rows,
    sum_wide,
    sum_send,
    sum_recv,
    local_sem,
    send_sem,
    recv_sem,
):
    my_group = lax.axis_index("group")
    my_shard = lax.axis_index("shard")

    def group_peer(k):
        return (lax.rem(my_group + k, N), my_shard)

    def shard_peer(k):
        return (my_group, lax.rem(my_shard + k, N))

    loads = []
    for number, (source, target) in enumerate(
        (
            (tokens_hbm, group_rows.at[0]),
            (kv_hbm, kv),
            (w_qkv_hbm, w_qkv),
            (w_out_hbm, w_out),
            (w_up_hbm, w_up),
            (w_gate_hbm, w_gate),
            (w_down_hbm, w_down),
        )
    ):
        copy = pltpu.make_async_copy(source, target, local_sem.at[number])
        copy.start()
        loads.append(copy)

    barrier = pltpu.get_barrier_semaphore()

    def greet(k, carry):
        pl.semaphore_signal(barrier, inc=1, device_id=group_peer(k), device_id_type=MESH)
        pl.semaphore_signal(barrier, inc=1, device_id=shard_peer(k), device_id_type=MESH)
        return carry

    lax.fori_loop(1, N, greet, 0)

    def push(source, target, peer, hop):
        def one(k, carry):
            pltpu.make_async_remote_copy(
                src_ref=source(k),
                dst_ref=target(k),
                send_sem=send_sem.at[hop],
                recv_sem=recv_sem.at[hop],
                device_id=peer(k),
                device_id_type=MESH,
            ).start()
            return carry

        lax.fori_loop(1, N, one, 0)

    def others(ref):
        return ref.at[pl.ds(1, N - 1)]

    def gather(rows, peer, hop):
        push(lambda k: rows.at[0], lambda k: rows.at[k], peer, hop)

    def give_back(source, target, hop):
        push(lambda k: source.at[k], lambda k: target.at[k], lambda k: shard_peer(N - k), hop)

    loads[0].wait()
    pl.semaphore_wait(barrier, 2 * (N - 1))

    gather(group_rows, group_peer, 0)

    rows2 = iota((2, 128), 0)
    lane = iota((1, 128), 1)
    length2 = jnp.where(rows2 == 0, lengths[0], lengths[1])
    in_length = iota((2, 128), 1) < length2
    keeper = jnp.where((keep_ref[...] == 1) & in_length, 1.0, 0.0)
    dropper = jnp.where((keep_ref[...] == 0) & in_length, 1.0, 0.0)
    lower = jnp.where(iota((128, 128), 0) <= iota((128, 128), 1), 1.0, 0.0).astype(BF16)
    position = jnp.dot(keeper.astype(BF16), lower, preferred_element_type=F32)
    place2 = jnp.where(keeper > 0.0, position - 1.0, -1.0)
    kept = jnp.sum(keeper, axis=1, keepdims=True)
    live2 = kept + jnp.where(jnp.sum(dropper, axis=1, keepdims=True) > 0.0, 1.0, 0.0)
    table_square = jnp.broadcast_to(table_ref[...].astype(F32), (WTAB, WTAB))
    table_column = jnp.sum(
        jnp.where(iota((WTAB, WTAB), 0) == iota((WTAB, WTAB), 1), table_square, 0.0),
        axis=1,
        keepdims=True,
    )
    target_row = iota((128, 128), 0).astype(F32)
    loads[1].wait()
    for j in range(2):
        hit = iota((WTAB, 128), 0) == index_ref[j : j + 1, :]
        weights = (
            jnp.sum(jnp.where(hit, table_column, 0.0), axis=0, keepdims=True)
            * dropper[j : j + 1, :]
        )
        placing = jnp.where(target_row == place2[j : j + 1, :], 1.0, 0.0)
        summing = jnp.where(target_row == kept[j : j + 1, :], weights, 0.0)
        mixing = (placing + summing).astype(BF16)
        for block in range(5):
            columns = slice(512 * block, 512 * block + 512)
            result = jnp.dot(mixing, kv[j, :, columns], preferred_element_type=F32)
            packed[8 * j : 8 * j + 8, :, columns] = result.astype(BF16).reshape(8, 16, 512)

    push(
        lambda k: packed.at[lax.rem(my_group + k, N)],
        lambda k: arrived.at[k],
        group_peer,
        1,
    )
    arrived[0] = packed[my_group]

    wait_for(others(group_rows), recv_sem.at[0])
    offset0 = offsets[0, 0]
    offset1 = offsets[0, 1]
    first = iota((2, D), 0) == 0
    own_tokens = group_rows[0].astype(F32)
    moved_tokens = jnp.where(
        first,
        group_rows[lax.rem(N - offset0, N)].astype(F32),
        group_rows[lax.rem(N - offset1, N)].astype(F32),
    )
    shard_rows[0] = moved_tokens.astype(BF16)
    gather(shard_rows, shard_peer, 2)

    def stack(rows):
        for k in range(N):
            lhs[2 * k : 2 * k + 2, :] = rows[k].astype(F32)
        return lhs[...].astype(BF16)

    def shifter(width, frame):
        shift = lax.rem(width * my_shard, 128)
        return jnp.where(
            iota((width, frame), 1) == iota((width, frame), 0) + shift, 1.0, 0.0
        ).astype(BF16)

    def spread_back(rows, weight, width, frame, send, recv, flat, hop):
        columns = jnp.dot(rows, weight, preferred_element_type=F32).astype(BF16)
        framed = jnp.dot(columns, shifter(width, frame), preferred_element_type=F32)
        for k in range(N):
            send[k] = framed[2 * k : 2 * k + 2, :]
        recv[0] = framed[0:2, :]
        give_back(send, recv, hop)
        flat[...] = jnp.zeros(flat.shape, F32)
        wait_for(others(recv), recv_sem.at[hop])
        for c in range(N):
            begin = 128 * ((width * c) // 128)
            flat[:, begin : begin + frame] += recv[lax.rem(c + N - my_shard, N)]

    loads[2].wait()
    wait_for(others(shard_rows), recv_sem.at[2])
    spread_back(stack(shard_rows), w_qkv[...], 240, 384, qkv_send, qkv_recv, qkv_flat, 3)

    head_mask = lax.shift_right_logical(iota((HEADS_PAD, D), 1), 6) == iota((HEADS_PAD, D), 0)
    eye = iota((HEADS_PAD, 128), 0) == iota((HEADS_PAD, 128), 1)
    scaling = qk_ref[...]
    score_scale = float(DH) ** 0.5

    def heads(row):
        masked = jnp.where(head_mask, jnp.broadcast_to(row, (HEADS_PAD, D)), 0.0)
        squares = jnp.sum(masked * masked, axis=1, keepdims=True)
        return (masked * lax.rsqrt(squares + EPSILON) * scaling).astype(BF16)

    home = lax.rem(my_group + offset1, N)
    partner_here = jnp.bitwise_xor(home, pair_bits[0])
    for j in range(2):
        queries = heads(qkv_flat[j : j + 1, 0:D])
        new_keys = heads(qkv_flat[j : j + 1, D : 2 * D])
        new_values = qkv_flat[j : j + 1, 2 * D : 3 * D]
        keys = packed[8 * j : 8 * j + 8, :, 0:D].reshape(128, D)
        values = packed[8 * j : 8 * j + 8, :, D : 2 * D].reshape(128, D)
        scores = score_scale * lax.dot_general(
            queries, keys, (((1,), (1,)), ((), ())), preferred_element_type=F32
        )
        fresh = score_scale * jnp.sum(
            queries.astype(F32) * new_keys.astype(F32), axis=1, keepdims=True
        )
        if j == 1:
            counted = jnp.full((HEADS_PAD, 1), home, jnp.int32) < partner_here
        else:
            counted = jnp.full((HEADS_PAD, 1), True)
        valid = jnp.broadcast_to(lane.astype(F32) < live2[j : j + 1, :], (HEADS_PAD, 128))
        highest = jnp.maximum(
            jnp.max(jnp.where(valid, scores, NEGATIVE), axis=1, keepdims=True),
            jnp.where(counted, fresh, NEGATIVE),
        )
        soft = jnp.where(valid, jnp.exp(jnp.where(valid, scores - highest, 0.0)), 0.0)
        fresh_weight = jnp.where(counted, jnp.exp(fresh - highest), 0.0)
        weight_sum = jnp.sum(soft, axis=1, keepdims=True) + fresh_weight
        weighted = jnp.dot(soft.astype(BF16), values, preferred_element_type=F32)
        weighted = weighted + fresh_weight.astype(BF16).astype(F32) * new_values
        if j == 0:
            weighted = weighted / weight_sum
        partial[0, :, j * D : j * D + D] = jnp.sum(
            jnp.where(head_mask, weighted, 0.0), axis=0, keepdims=True
        )
        if j == 1:
            partial[0, :, 2 * D : 2 * D + 128] = jnp.sum(
                jnp.where(eye, highest, 0.0), axis=0, keepdims=True
            )
            partial[0, :, 2 * D + 128 : 2 * D + 256] = jnp.sum(
                jnp.where(eye, weight_sum, 0.0), axis=0, keepdims=True
            )

    gather(partial, group_peer, 4)

    wait_for(others(arrived), recv_sem.at[1])
    my_offset = offsets[0, lax.div(my_group, 8)]
    for m in range(N):
        staged[m] = arrived[lax.rem(my_offset + N - m, N)]
    landing = cache_out.at[
        lax.div(my_group, 8), pl.ds(pl.multiple_of(16 * lax.rem(my_group, 8), 16), 16), :
    ]
    push(lambda k: staged.at[k], lambda k: landing, group_peer, 5)
    own_chunk = pltpu.make_async_copy(staged.at[0], landing, local_sem.at[7])
    own_chunk.start()

    wait_for(others(partial), recv_sem.at[4])
    partner = jnp.bitwise_xor(my_group, pair_bits[0])
    mine = partial[offset1]
    other = partial[lax.rem(my_group - partner + offset1 + N, N)]
    my_high = mine[:, 2 * D : 2 * D + 128]
    other_high = other[:, 2 * D : 2 * D + 128]
    merged = jnp.maximum(my_high, other_high)
    my_factor = jnp.exp(my_high - merged)
    other_factor = jnp.exp(other_high - merged)
    long_sum = (
        mine[:, 2 * D + 128 : 2 * D + 256] * my_factor
        + other[:, 2 * D + 128 : 2 * D + 256] * other_factor
    )

    def by_column(row):
        column = jnp.sum(
            jnp.where(eye, jnp.broadcast_to(row, (HEADS_PAD, 128)), 0.0), axis=1, keepdims=True
        )
        return jnp.sum(jnp.where(head_mask, column, 0.0), axis=0, keepdims=True)

    long_row = mine[:, D : 2 * D] * by_column(my_factor / long_sum) + other[
        :, D : 2 * D
    ] * by_column(other_factor / long_sum)
    short_row = partial[offset0][:, 0:D]
    attended = jnp.where(
        first, jnp.broadcast_to(short_row, (2, D)), jnp.broadcast_to(long_row, (2, D))
    )
    attended_rows[0] = attended.astype(BF16)
    gather(attended_rows, shard_peer, 6)

    loads[3].wait()
    wait_for(others(attended_rows), recv_sem.at[6])
    spread_back(stack(attended_rows), w_out[...], 80, 256, out_send, out_recv, out_flat, 7)
    attention_out = out_flat[:, 0:D]
    mixed = rms_normal(
        own_tokens + attn_rate_ref[...] * (rms_normal(attention_out) - own_tokens)
    )
    mixed_rows[0] = mixed.astype(BF16)
    gather(mixed_rows, shard_peer, 8)

    loads[4].wait()
    loads[5].wait()
    loads[6].wait()
    wait_for(others(mixed_rows), recv_sem.at[8])
    rows = stack(mixed_rows)
    up = jnp.dot(rows, w_up[...], preferred_element_type=F32) * up_scale_ref[...]
    gate = jnp.dot(rows, w_gate[...], preferred_element_type=F32) * (
        gate_scale_ref[...] * float(D) ** 0.5
    )
    inner = (up * (gate / (1.0 + jnp.exp(-gate)))).astype(BF16)
    sum_wide[...] = jnp.dot(inner, w_down[...], preferred_element_type=F32)
    for k in range(N):
        sum_send[k] = sum_wide[2 * k : 2 * k + 2, :].astype(BF16)
    sum_recv[0] = sum_send[0]
    give_back(sum_send, sum_recv, 9)
    wait_for(others(sum_recv), recv_sem.at[9])
    mlp_out = sum_recv[0].astype(F32)
    for k in range(1, N):
        mlp_out = mlp_out + sum_recv[k].astype(F32)
    hidden_out[...] = rms_normal(
        mixed + mlp_rate_ref[...] * (rms_normal(mlp_out) - mixed)
    ).astype(BF16)

    fifteen = pl.ds(1, N - 1)
    wait_for(others(staged), recv_sem.at[5])
    own_chunk.wait()
    for hop, ref in enumerate(
        (
            group_rows,
            arrived,
            shard_rows,
            qkv_recv,
            partial,
            staged,
            attended_rows,
            out_recv,
            mixed_rows,
            sum_recv,
        )
    ):
        wait_for(others(ref), send_sem.at[hop])


def per_device(
    tokens,
    kv_cache,
    keep_list,
    lengths,
    merge_index,
    merge_table,
    move_offset,
    pair_mask,
    w_qkv,
    w_out,
    w_up,
    w_gate,
    w_down,
    qk_scale,
    attn_rate,
    mlp_rate,
    up_scale,
    gate_scale,
):
    smem = pl.BlockSpec(memory_space=pltpu.SMEM)
    vmem = pl.BlockSpec(memory_space=pltpu.VMEM)
    anywhere = pl.BlockSpec(memory_space=pl.ANY)

    def row(vector):
        return vector.reshape(1, -1)

    return pl.pallas_call(
        layer_kernel,
        out_shape=(
            jax.ShapeDtypeStruct((2, D), BF16),
            jax.ShapeDtypeStruct((2, 128, 2 * D), BF16),
        ),
        in_specs=[smem] * 3 + [vmem] * 8 + [anywhere] * 7,
        out_specs=(vmem, anywhere),
        scratch_shapes=[
            pltpu.VMEM((2, 128, 2 * D), BF16),
            pltpu.VMEM((D, 240), BF16),
            pltpu.VMEM((D, 80), BF16),
            pltpu.VMEM((D, 320), BF16),
            pltpu.VMEM((D, 320), BF16),
            pltpu.VMEM((320, D), BF16),
            pltpu.VMEM((N, 16, 2 * D), BF16),
            pltpu.VMEM((N, 16, 2 * D), BF16),
            pltpu.VMEM((N, 16, 2 * D), BF16),
            pltpu.VMEM((N, 2, D), BF16),
            pltpu.VMEM((N, 2, D), BF16),
            pltpu.VMEM((2 * N, D), F32),
            pltpu.VMEM((N, 2, 384), F32),
            pltpu.VMEM((N, 2, 384), F32),
            pltpu.VMEM((2, 3 * D + 128), F32),
            pltpu.VMEM((N, 1, 2 * D + 256), F32),
            pltpu.VMEM((N, 2, D), BF16),
            pltpu.VMEM((N, 2, 256), F32),
            pltpu.VMEM((N, 2, 256), F32),
            pltpu.VMEM((2, D + 128), F32),
            pltpu.VMEM((N, 2, D), BF16),
            pltpu.VMEM((2 * N, D), F32),
            pltpu.VMEM((N, 2, D), BF16),
            pltpu.VMEM((N, 2, D), BF16),
            pltpu.SemaphoreType.DMA((8,)),
            pltpu.SemaphoreType.DMA((10,)),
            pltpu.SemaphoreType.DMA((10,)),
        ],
        compiler_params=pltpu.CompilerParams(
            collective_id=0, has_side_effects=True, vmem_limit_bytes=40 << 20
        ),
    )(
        lengths,
        move_offset,
        pair_mask,
        keep_list,
        merge_index,
        row(merge_table),
        row(qk_scale),
        row(attn_rate),
        row(mlp_rate),
        row(up_scale),
        row(gate_scale),
        tokens,
        kv_cache,
        w_qkv,
        w_out,
        w_up,
        w_gate,
        w_down,
    )


def solution(mesh):
    return jax.shard_map(
        per_device,
        mesh=mesh,
        in_specs=(
            P(("group", "shard"), None),
            P(("group", "shard"), None, None),
            P(("group", "shard"), None),
            P(("group", "shard")),
            P(("group", "shard"), None),
            P(),
            P("shard", None),
            P("shard"),
            P(None, "shard"),
            P(None, "shard"),
            P(None, "shard"),
            P(None, "shard"),
            P("shard", None),
            P(),
            P(),
            P(),
            P("shard"),
            P("shard"),
        ),
        out_specs=(P(("group", "shard"), None), P(("group", "shard"), None, None)),
        check_vma=False,
    )
```

time: 550 us -> 91.2 us (0.17)
  waiting for transfers between devices: 328 us -> 0 us
  blocking collectives: 105 us -> 0 us
  Pallas kernels: 0 us -> 77 us
  matrix products: 33.4 us -> 0 us
  starting transfers between devices: 31.7 us -> 0 us
  local copies, waits for them, and re-layouts: 26.5 us -> 12.3 us
  between operations: 15.6 us -> 1.51 us
  other arithmetic: 8.59 us -> 0 us
    all_to_all x4 -> x0, waiting for transfers between devices: 233 us -> none  [the longest x1 226 us: per_device(): lax.all_to_all(outgoing, 'group', split_axis=0, concat_axis=0, tiled=True)]
    all_gather x6 -> x0, blocking collectives: 105 us -> none  [the longest x2 39.3 us: spread_columns(): lax.all_gather(row_block, 'shard', axis=0, tiled=True)]
    unnamed x2 -> x0, waiting for transfers between devices: 95.2 us -> none
    pallas_call x0 -> x1, Pallas kernels: none -> 77 us  [per_device(): pl.pallas_call(layer_kernel, out_shape=(jax.ShapeDtypeStruct((2, D), BF16...]
    dot_general x11 -> x0, matrix products: 33.4 us -> none  [the longest x1 15.7 us: per_device(): jnp.einsum('jp,prc->jrc', picker, incoming, preferred_element_type=jnp.fl...]
    all_to_all x4 -> x0, starting transfers between devices: 31.6 us -> none  [the longest x1 12.6 us: per_device(): lax.all_to_all(outgoing, 'group', split_axis=0, concat_axis=0, tiled=True)]
    convert_element_type x4 -> x0, local copies, waits for them, and re-layouts: 13.9 us -> none  [the longest x1 13.7 us: per_device(): jnp.einsum('pj,jrc->prc', sender, packed, preferred_element_type=jnp.floa...]
    slice x4 -> x0, local copies, waits for them, and re-layouts: 6.58 us -> none  [the longest x2 3.62 us: per_device(): moved_cache[:, :, model_width:].reshape(slot_count, context, head_count, DH)]
  transfers between devices with their start and end apart: 5 -> 0, of which waited for: 3 -> 0; matrix products, arithmetic and copies ran while one was open for 5% -> 0% of each run, Pallas kernels for 0% -> 0%
where the time goes in v1:
time: 91.2 us; the launch traced here: 90.8 us
  Pallas kernels  77 us (84%)
  local copies, waits for them, and re-layouts  12.3 us (13%)
  between operations  1.51 us (2%)
    pallas_call x1, Pallas kernels, per_device(): pl.pallas_call(layer_kernel, out_shape=(jax.ShapeDtypeStruct((2, D), BF16...  77 us
    unnamed x24, local copies, waits for them, and re-layouts  8.82 us
    reshape x5, local copies, waits for them, and re-layouts, row(): return vector.reshape(1, -1)  3.47 us

profile of v1, /device:TPU:1, one launch (start us, length us, event | category | flops | bytes accessed | tf_op | source)
XLA Modules:
  0.0 90.8 jit_solution(17718657480790765818)
XLA Ops:
  0.6 0.0 copy-start.8
  1.4 0.7 reshape.26.up_scale_ref
  2.0 0.7 reshape.27.gate_scale_ref
  2.7 0.7 reshape.23.qk_ref
  3.4 0.7 reshape.24.attn_rate_ref
  4.1 0.7 reshape.25.mlp_rate_ref
  4.8 1.1 %copy.21.w_out_hbm = bf16[1280,80]{1,0:T(8,128)(2,1)S(1)} copy(bf16[1280,80]{0,1:T(8,128)(2,1)} %param.27) | data formatting | bytes 409600 | tf_op args[9]
  6.0 1.3 %copy.20.w_qkv_hbm = bf16[1280,240]{1,0:T(8,128)(2,1)S(1)} copy(bf16[1280,240]{0,1:T(8,128)(2,1)} %param.26) | data formatting | bytes 1228800 | tf_op args[8]
  7.3 0.0 copy-done.8
  7.3 0.6 copy.22.w_up_hbm
  8.0 0.0 copy-start.2
  8.0 0.0 copy-start.3
  8.0 0.0 copy-start.4
  8.0 0.0 copy-start.5
  8.0 0.0 copy-start.6
  8.0 0.0 copy-start.7
  8.0 1.6 %copy.23.w_gate_hbm = bf16[1280,320]{1,0:T(8,128)(2,1)S(1)} copy(bf16[1280,320]{0,1:T(8,128)(2,1)} %param.29) | data formatting | bytes 1638400 | tf_op args[11]
  9.6 0.0 copy-done.2
  9.6 0.0 copy-done.3
  9.6 0.0 copy-done.4
  9.6 0.0 copy-done.5
  9.6 0.0 copy-done.6
  9.7 0.0 copy-done.7
  9.7 0.0 copy-start
  9.7 1.3 %copy-done = bf16[2,128,2560]{2,1,0:T(8,128)(2,1)S(1)} copy-done((bf16[2,128,2560]{2,1,0:T(8,128)(2,1)S(1)}, bf16[2,128,2560]{2,1,0:T(8,128)(2,1)}, u32[]{:S(2)}) %copy-start) | copy-done | bytes 1310744
  11.0 0.0 copy-start.1
  11.0 1.1 %copy-done.1 = bf16[320,1280]{1,0:T(8,128)(2,1)S(1)} copy-done((bf16[320,1280]{1,0:T(8,128)(2,1)S(1)}, bf16[320,1280]{1,0:T(8,128)(2,1)}, u32[]{:S(2)}) %copy-start.1) | copy-done | bytes 819224
  12.1 77.0 %shard_map.185 = (bf16[2,1280]{1,0:T(2,128)(2,1)S(1)}, bf16[2,128,2560]{2,1,0:T(8,128)(2,1)S(1)}) custom-call(s32[2]{0:T(128)S(1)} %copy-done.5, s32[1,2]{1,0:T(1,128)S(1)} %copy-done.6, s32[1]{0:T(128)S(6)} %copy.26.pair_bits, s32[2,128]{1,0:T(2,128)S(1)} %copy-done.3, s32[2,128]{1,0:T(2,128)S(1)} %copy-done.4, bf16[1,16]{1,0:T(2,128)(2,1)S(1)} %bitcast.1, ...), custom_call_target="tpu_custom_call" | custom-call | tf_op jit(solution)/shard_map/pallas_call | solution.py:402
  89.1 0.6 copy.27
  89.7 1.1 %copy.28 = bf16[2,128,2560]{2,1,0:T(8,128)(2,1)} copy(bf16[2,128,2560]{2,1,0:T(8,128)(2,1)S(1)} %get-tuple-element.5) | data formatting | bytes 2621440
Async XLA Ops:
  0.6 6.7 %copy-start.8 = (bf16[1280,320]{0,1:T(8,128)(2,1)S(1)}, bf16[1280,320]{0,1:T(8,128)(2,1)}, u32[]{:S(2)}) copy-start(bf16[1280,320]{0,1:T(8,128)(2,1)} %param.28) | copy-start | bytes 2457604
  8.0 1.7 %copy-start.2 = (bf16[2,1280]{1,0:T(2,128)(2,1)S(1)}, bf16[2,1280]{1,0:T(2,128)(2,1)}, u32[]{:S(2)}) copy-start(bf16[2,1280]{1,0:T(2,128)(2,1)} %tokens_hbm.1) | copy-start | bytes 15364
  8.0 1.7 %copy-start.3 = (s32[2,128]{1,0:T(2,128)S(1)}, s32[2,128]{1,0:T(2,128)}, u32[]{:S(2)}) copy-start(s32[2,128]{1,0:T(2,128)} %keep_ref.1) | copy-start | bytes 3076
  8.0 1.7 %copy-start.4 = (s32[2,128]{1,0:T(2,128)S(1)}, s32[2,128]{1,0:T(2,128)}, u32[]{:S(2)}) copy-start(s32[2,128]{1,0:T(2,128)} %index_ref.1) | copy-start | bytes 3076
  8.0 1.6 %copy-start.5 = (s32[2]{0:T(128)S(1)}, s32[2]{0:T(128)}, u32[]{:S(2)}) copy-start(s32[2]{0:T(128)} %lengths.1) | copy-start | bytes 28
  8.0 1.6 %copy-start.6 = (s32[1,2]{1,0:T(1,128)S(1)}, s32[1,2]{1,0:T(1,128)}, u32[]{:S(2)}) copy-start(s32[1,2]{1,0:T(1,128)} %offsets.1) | copy-start | bytes 28
  8.0 1.6 %copy-start.7 = (bf16[16]{0:T(256)(128)(2,1)S(1)}, bf16[16]{0:T(256)(128)(2,1)}, u32[]{:S(2)}) copy-start(bf16[16]{0:T(256)(128)(2,1)} %param.23) | copy-start | bytes 100
  9.7 1.3 %copy-start = (bf16[2,128,2560]{2,1,0:T(8,128)(2,1)S(1)}, bf16[2,128,2560]{2,1,0:T(8,128)(2,1)}, u32[]{:S(2)}) copy-start(bf16[2,128,2560]{2,1,0:T(8,128)(2,1)} %kv_hbm.1) | copy-start | bytes 3932164
  11.0 1.1 %copy-start.1 = (bf16[320,1280]{1,0:T(8,128)(2,1)S(1)}, bf16[320,1280]{1,0:T(8,128)(2,1)}, u32[]{:S(2)}) copy-start(bf16[320,1280]{1,0:T(8,128)(2,1)} %w_down_hbm.1) | copy-start | bytes 2457604

commit v2 on v1

v2 whole, which is shorter than its diff:
```python
import functools
import math

import jax
import jax.numpy as jnp
from jax import lax
from jax.experimental import pallas as pl
from jax.experimental.pallas import tpu as pltpu
from jax.sharding import PartitionSpec as P

DH = 64
WTAB = 16
N = 16
D = 1280
PARTS = 2
WIDE = 2 * D // PARTS
KEY_PARTS = PARTS // 2
HOPS = 10
HEADS_PAD = 32
EPSILON = 1e-06
NEGATIVE = -1e30
MESH = pl.DeviceIdType.MESH
F32 = jnp.float32
BF16 = jnp.bfloat16


def iota(shape, axis):
    return lax.broadcasted_iota(jnp.int32, shape, axis)


def rms_normal(vector):
    return vector * lax.rsqrt(jnp.mean(vector * vector, axis=-1, keepdims=True) + EPSILON)


def times_transposed(rows, weight):
    return lax.dot_general(rows, weight, (((1,), (1,)), ((), ())), preferred_element_type=F32)


def wait_for(ref, sem):
    pltpu.make_async_copy(ref, ref, sem).wait()


def layer_kernel(
    lengths,
    offsets,
    pair_bits,
    keep_ref,
    index_ref,
    table_ref,
    qk_ref,
    attn_rate_ref,
    mlp_rate_ref,
    up_scale_ref,
    gate_scale_ref,
    tokens_hbm,
    kv_hbm,
    w_qkv_hbm,
    w_out_hbm,
    w_up_hbm,
    w_gate_hbm,
    w_down_hbm,
    hidden_out,
    cache_out,
    kv,
    w_qkv,
    w_out,
    w_up,
    w_gate,
    w_down,
    packed,
    arrived,
    staged,
    group_rows,
    shard_rows,
    lhs,
    qkv_send,
    qkv_recv,
    qkv_flat,
    partial_wide,
    partial,
    attended_rows,
    out_send,
    out_recv,
    out_flat,
    mixed_rows,
    sum_wide,
    sum_send,
    sum_recv,
    local_sem,
    send_sem,
    recv_sem,
):
    my_group = lax.axis_index("group")
    my_shard = lax.axis_index("shard")

    def group_peer(k):
        return (lax.rem(my_group + k, N), my_shard)

    def shard_peer(k):
        return (my_group, lax.rem(my_shard + k, N))

    loads = []
    for number, (source, target) in enumerate(
        (
            (tokens_hbm, group_rows.at[0]),
            (kv_hbm, kv),
            (w_qkv_hbm, w_qkv),
            (w_out_hbm, w_out),
            (w_up_hbm, w_up),
            (w_gate_hbm, w_gate),
            (w_down_hbm, w_down),
        )
    ):
        copy = pltpu.make_async_copy(source, target, local_sem.at[number])
        copy.start()
        loads.append(copy)

    barrier = pltpu.get_barrier_semaphore()

    def greet(k, carry):
        pl.semaphore_signal(barrier, inc=1, device_id=group_peer(k), device_id_type=MESH)
        pl.semaphore_signal(barrier, inc=1, device_id=shard_peer(k), device_id_type=MESH)
        return carry

    lax.fori_loop(1, N, greet, 0)

    def push(source, target, peer, hop, stride=1):
        def one(k):
            pltpu.make_async_remote_copy(
                src_ref=source(k),
                dst_ref=target(k),
                send_sem=send_sem.at[hop],
                recv_sem=recv_sem.at[hop],
                device_id=peer(k),
                device_id_type=MESH,
            ).start()

        one(N // 2)

        def pair(step, carry):
            one(N // 2 - stride * step)
            one(N // 2 + stride * step)
            return carry

        lax.fori_loop(1, N // 2 // stride, pair, 0)

    def others(ref):
        return ref.at[pl.ds(1, N - 1)]

    def gather(rows, peer, hop):
        push(lambda k: rows.at[0], lambda k: rows.at[k], peer, hop)

    sibling = my_group + 1 - 2 * lax.rem(my_group, 2)

    def gather_group(rows, hop):
        push(lambda k: rows.at[0], lambda k: rows.at[lax.div(k, 2)], group_peer, hop, 2)

    def relay_group(rows, hop, relay_hop):
        wait_for(rows.at[pl.ds(1, N // 2 - 1)], recv_sem.at[hop])
        pltpu.make_async_remote_copy(
            src_ref=rows.at[pl.ds(0, N // 2)],
            dst_ref=rows.at[pl.ds(N // 2, N // 2)],
            send_sem=send_sem.at[relay_hop],
            recv_sem=recv_sem.at[relay_hop],
            device_id=(sibling, my_shard),
            device_id_type=MESH,
        ).start()
        wait_for(rows.at[pl.ds(N // 2, N // 2)], recv_sem.at[relay_hop])

    def slot_of(group):
        back = lax.rem(my_group - group + 2 * N, N)
        sibling_back = lax.rem(sibling - group + 2 * N, N)
        odd = lax.rem(back, 2)
        return (1 - odd) * lax.div(back, 2) + odd * (N // 2 + lax.div(sibling_back, 2))

    def give_back(source, target, hop):
        push(lambda k: source.at[k], lambda k: target.at[k], lambda k: shard_peer(N - k), hop)

    rows2 = iota((2, 128), 0)
    lane = iota((1, 128), 1)
    length2 = jnp.where(rows2 == 0, lengths[0], lengths[1])
    in_length = iota((2, 128), 1) < length2
    keeper = jnp.where((keep_ref[...] == 1) & in_length, 1.0, 0.0)
    dropper = jnp.where((keep_ref[...] == 0) & in_length, 1.0, 0.0)
    lower = jnp.where(iota((128, 128), 0) <= iota((128, 128), 1), 1.0, 0.0).astype(BF16)
    position = jnp.dot(keeper.astype(BF16), lower, preferred_element_type=F32)
    place2 = jnp.where(keeper > 0.0, position - 1.0, -1.0)
    kept = jnp.sum(keeper, axis=1, keepdims=True)
    live2 = kept + jnp.where(jnp.sum(dropper, axis=1, keepdims=True) > 0.0, 1.0, 0.0)
    table_square = jnp.broadcast_to(table_ref[...].astype(F32), (WTAB, WTAB))
    table_column = jnp.sum(
        jnp.where(iota((WTAB, WTAB), 0) == iota((WTAB, WTAB), 1), table_square, 0.0),
        axis=1,
        keepdims=True,
    )
    target_row = iota((128, 128), 0).astype(F32)
    loads[1].wait()
    for j in range(2):
        hit = iota((WTAB, 128), 0) == index_ref[j : j + 1, :]
        weights = (
            jnp.sum(jnp.where(hit, table_column, 0.0), axis=0, keepdims=True)
            * dropper[j : j + 1, :]
        )
        placing = jnp.where(target_row == place2[j : j + 1, :], 1.0, 0.0)
        summing = jnp.where(target_row == kept[j : j + 1, :], weights, 0.0)
        mixing = (placing + summing).astype(BF16)
        for part in range(PARTS):
            columns = slice(WIDE * part, WIDE * part + WIDE)
            result = jnp.dot(mixing, kv[j, :, columns], preferred_element_type=F32)
            packed[part, 8 * j : 8 * j + 8] = result.astype(BF16).reshape(8, 16, WIDE)

    loads[0].wait()
    pl.semaphore_wait(barrier, 2 * (N - 1))

    gather_group(group_rows, 0)

    def spread_cache(part):
        push(
            lambda k: packed.at[part, lax.rem(my_group + k, N)],
            lambda k: arrived[part].at[k],
            group_peer,
            HOPS + part,
        )
        arrived[part][0] = packed[part, my_group]

    for part in range(PARTS):
        spread_cache(part)

    landing_slot = lax.div(my_group, 8)
    landing_rows = pl.ds(pl.multiple_of(16 * lax.rem(my_group, 8), 16), 16)
    my_offset = offsets[0, landing_slot]
    own_chunks = []

    def deliver_cache(part):
        wait_for(others(arrived[part]), recv_sem.at[HOPS + part])
        for m in range(N):
            staged[part, m] = arrived[part][lax.rem(my_offset + N - m, N)]
        landing = cache_out.at[landing_slot, landing_rows, pl.ds(WIDE * part, WIDE)]
        push(
            lambda k: staged.at[part, k], lambda k: landing, group_peer, HOPS + PARTS + part
        )
        own_chunk = pltpu.make_async_copy(staged.at[part, 0], landing, local_sem.at[7 + part])
        own_chunk.start()
        own_chunks.append(own_chunk)

    relay_group(group_rows, 0, 8)
    offset0 = offsets[0, 0]
    offset1 = offsets[0, 1]
    first = iota((2, D), 0) == 0
    own_tokens = group_rows[0].astype(F32)
    moved_tokens = jnp.where(
        first,
        group_rows[slot_of(my_group + offset0)].astype(F32),
        group_rows[slot_of(my_group + offset1)].astype(F32),
    )
    shard_rows[0] = moved_tokens.astype(BF16)
    gather(shard_rows, shard_peer, 1)

    def stack(rows):
        for k in range(N):
            lhs[2 * k : 2 * k + 2, :] = rows[k].astype(F32)
        return lhs[...].astype(BF16)

    def shifter(width, frame):
        shift = lax.rem(width * my_shard, 128)
        return jnp.where(
            iota((width, frame), 1) == iota((width, frame), 0) + shift, 1.0, 0.0
        ).astype(BF16)

    def spread_back(rows, weight, width, frame, send, recv, flat, hop):
        columns = times_transposed(rows, weight).astype(BF16)
        framed = jnp.dot(columns, shifter(width, frame), preferred_element_type=F32)
        for k in range(N):
            send[k] = framed[2 * k : 2 * k + 2, :]
        recv[0] = framed[0:2, :]
        give_back(send, recv, hop)
        flat[...] = jnp.zeros(flat.shape, F32)
        wait_for(others(recv), recv_sem.at[hop])
        for c in range(N):
            begin = 128 * ((width * c) // 128)
            flat[:, begin : begin + frame] += recv[lax.rem(c + N - my_shard, N)]

    loads[2].wait()
    wait_for(others(shard_rows), recv_sem.at[1])
    spread_back(stack(shard_rows), w_qkv[...], 240, 384, qkv_send, qkv_recv, qkv_flat, 2)

    head_mask = lax.shift_right_logical(iota((HEADS_PAD, D), 1), 6) == iota((HEADS_PAD, D), 0)
    stat_row = iota((HEADS_PAD, 128), 0)
    stat_column = iota((HEADS_PAD, 128), 1)
    stat_lane = stat_column == stat_row
    stat_lane1 = stat_column == stat_row + HEADS_PAD
    stat_lane2 = stat_column == stat_row + 2 * HEADS_PAD
    stat_any = stat_lane | stat_lane1 | stat_lane2
    scaling = qk_ref[...][None, :]
    score_scale = float(DH) ** 0.5

    def heads(row):
        masked = jnp.where(head_mask, jnp.broadcast_to(row, (HEADS_PAD, D)), 0.0)
        squares = jnp.sum(masked * masked, axis=1, keepdims=True)
        return (masked * lax.rsqrt(squares + EPSILON) * scaling).astype(BF16)

    home = lax.rem(my_group + offset1, N)
    partner_here = jnp.bitwise_xor(home, pair_bits[0, 0])
    for j in range(2):
        queries = heads(qkv_flat[j : j + 1, 0:D])
        new_keys = heads(qkv_flat[j : j + 1, D : 2 * D])
        new_values = qkv_flat[j : j + 1, 2 * D : 3 * D]
        scores = sum(
            times_transposed(
                queries[:, WIDE * part : WIDE * part + WIDE],
                packed[part, 8 * j : 8 * j + 8].reshape(128, WIDE),
            )
            for part in range(KEY_PARTS)
        )
        scores = score_scale * scores
        fresh = score_scale * jnp.sum(
            queries.astype(F32) * new_keys.astype(F32), axis=1, keepdims=True
        )
        if j == 1:
            counted = jnp.full((HEADS_PAD, 1), home, jnp.int32) < partner_here
        else:
            counted = jnp.full((HEADS_PAD, 1), True)
        valid = jnp.broadcast_to(lane.astype(F32) < live2[j : j + 1, :], (HEADS_PAD, 128))
        highest = jnp.maximum(
            jnp.max(jnp.where(valid, scores, NEGATIVE), axis=1, keepdims=True),
            jnp.where(counted, fresh, NEGATIVE),
        )
        soft = jnp.where(valid, jnp.exp(jnp.where(valid, scores - highest, 0.0)), 0.0)
        fresh_weight = jnp.where(counted, jnp.exp(fresh - highest), 0.0)
        weight_sum = jnp.sum(soft, axis=1, keepdims=True) + fresh_weight
        fresh_low = fresh_weight.astype(BF16).astype(F32)
        for part in range(KEY_PARTS):
            columns = slice(WIDE * part, WIDE * part + WIDE)
            values = packed[KEY_PARTS + part, 8 * j : 8 * j + 8].reshape(128, WIDE)
            weighted = jnp.dot(soft.astype(BF16), values, preferred_element_type=F32)
            weighted = weighted + fresh_low * new_values[:, columns]
            partial_wide[j : j + 1, columns] = jnp.sum(
                jnp.where(head_mask[:, columns], weighted / weight_sum, 0.0),
                axis=0,
                keepdims=True,
            )
    total = highest + jnp.log(weight_sum)
    piece0 = total.astype(BF16).astype(F32)
    piece1 = (total - piece0).astype(BF16).astype(F32)
    piece2 = total - piece0 - piece1
    pieces = jnp.where(stat_lane, piece0, 0.0)
    pieces = pieces + jnp.where(stat_lane1, piece1, 0.0)
    pieces = pieces + jnp.where(stat_lane2, piece2, 0.0)
    partial_wide[0:1, D : D + 128] = jnp.zeros((1, 128), F32)
    partial_wide[1:2, D : D + 128] = jnp.sum(pieces, axis=0, keepdims=True)
    partial[0] = partial_wide[...].astype(BF16)

    gather_group(partial, 3)

    deliver_cache(0)

    relay_group(partial, 3, 9)
    partner = jnp.bitwise_xor(my_group, pair_bits[0, 0])
    mine = partial[slot_of(my_group - offset1)].astype(F32)[1:2, :]
    other = partial[slot_of(partner - offset1)].astype(F32)[1:2, :]

    def total_of(row):
        pieces = jnp.broadcast_to(row[:, D : D + 128], (HEADS_PAD, 128))
        return jnp.sum(jnp.where(stat_any, pieces, 0.0), axis=1, keepdims=True)

    def by_column(column):
        return jnp.sum(jnp.where(head_mask, column, 0.0), axis=0, keepdims=True)

    my_total = total_of(mine)
    other_total = total_of(other)
    merged = jnp.maximum(my_total, other_total)
    my_factor = jnp.exp(my_total - merged)
    other_factor = jnp.exp(other_total - merged)
    both = my_factor + other_factor
    long_row = mine[:, 0:D] * by_column(my_factor / both) + other[:, 0:D] * by_column(
        other_factor / both
    )
    short_row = partial[slot_of(my_group - offset0)].astype(F32)[0:1, 0:D]
    attended = jnp.where(
        first, jnp.broadcast_to(short_row, (2, D)), jnp.broadcast_to(long_row, (2, D))
    )
    attended_rows[0] = attended.astype(BF16)
    gather(attended_rows, shard_peer, 4)
    for part in range(1, PARTS):
        deliver_cache(part)

    loads[3].wait()
    wait_for(others(attended_rows), recv_sem.at[4])
    spread_back(stack(attended_rows), w_out[...], 80, 256, out_send, out_recv, out_flat, 5)
    attention_out = out_flat[:, 0:D]
    mixed = rms_normal(
        own_tokens + attn_rate_ref[...][None, :] * (rms_normal(attention_out) - own_tokens)
    )
    mixed_rows[0] = mixed.astype(BF16)
    gather(mixed_rows, shard_peer, 6)

    loads[4].wait()
    loads[5].wait()
    loads[6].wait()
    wait_for(others(mixed_rows), recv_sem.at[6])
    rows = stack(mixed_rows)
    up = times_transposed(rows, w_up[...]) * up_scale_ref[...][None, :]
    gate = times_transposed(rows, w_gate[...]) * (
        gate_scale_ref[...][None, :] * float(D) ** 0.5
    )
    inner = (up * (gate / (1.0 + jnp.exp(-gate)))).astype(BF16)
    sum_wide[...] = jnp.dot(inner, w_down[...], preferred_element_type=F32)
    for k in range(N):
        sum_send[k] = sum_wide[2 * k : 2 * k + 2, :].astype(BF16)
    sum_recv[0] = sum_send[0]
    give_back(sum_send, sum_recv, 7)
    wait_for(others(sum_recv), recv_sem.at[7])
    mlp_out = sum_recv[0].astype(F32)
    for k in range(1, N):
        mlp_out = mlp_out + sum_recv[k].astype(F32)
    hidden_out[...] = rms_normal(
        mixed + mlp_rate_ref[...][None, :] * (rms_normal(mlp_out) - mixed)
    ).astype(BF16)

    for part in range(PARTS):
        wait_for(others(staged.at[part]), recv_sem.at[HOPS + PARTS + part])
        own_chunks[part].wait()
    half = pl.ds(N // 2, N // 2)
    most = pl.ds(1, N // 2 - 1)
    sent = (
        [
            group_rows.at[most],
            others(shard_rows),
            others(qkv_recv),
            partial.at[most],
            others(attended_rows),
            others(out_recv),
            others(mixed_rows),
            others(sum_recv),
            group_rows.at[half],
            partial.at[half],
        ]
        + [others(arrived[part]) for part in range(PARTS)]
        + [others(staged.at[part]) for part in range(PARTS)]
    )
    for hop, ref in enumerate(sent):
        wait_for(ref, send_sem.at[hop])


def per_device(
    tokens,
    kv_cache,
    keep_list,
    lengths,
    merge_index,
    merge_table,
    move_offset,
    pair_mask,
    w_qkv,
    w_out,
    w_up,
    w_gate,
    w_down,
    qk_scale,
    attn_rate,
    mlp_rate,
    up_scale,
    gate_scale,
):
    smem = pl.BlockSpec(memory_space=pltpu.SMEM)
    vmem = pl.BlockSpec(memory_space=pltpu.VMEM)
    hbm = pl.BlockSpec(memory_space=pltpu.HBM)

    return pl.pallas_call(
        layer_kernel,
        out_shape=(
            pltpu.VMEM((2, D), BF16),
            pltpu.VMEM((2, 128, 2 * D), BF16),
        ),
        in_specs=[smem] * 3 + [vmem] * 8 + [hbm] * 7,
        out_specs=(vmem, pl.BlockSpec(memory_space=pl.ANY)),
        scratch_shapes=[
            pltpu.VMEM((2, 128, 2 * D), BF16),
            pltpu.VMEM((240, D), BF16),
            pltpu.VMEM((80, D), BF16),
            pltpu.VMEM((320, D), BF16),
            pltpu.VMEM((320, D), BF16),
            pltpu.VMEM((320, D), BF16),
            pltpu.VMEM((PARTS, N, 16, WIDE), BF16),
            [pltpu.VMEM((N, 16, WIDE), BF16)] * PARTS,
            pltpu.VMEM((PARTS, N, 16, WIDE), BF16),
            pltpu.VMEM((N, 2, D), BF16),
            pltpu.VMEM((N, 2, D), BF16),
            pltpu.VMEM((2 * N, D), F32),
            pltpu.VMEM((N, 2, 384), F32),
            pltpu.VMEM((N, 2, 384), F32),
            pltpu.VMEM((2, 3 * D + 128), F32),
            pltpu.VMEM((2, D + 128), F32),
            pltpu.VMEM((N, 2, D + 128), BF16),
            pltpu.VMEM((N, 2, D), BF16),
            pltpu.VMEM((N, 2, 256), F32),
            pltpu.VMEM((N, 2, 256), F32),
            pltpu.VMEM((2, D + 128), F32),
            pltpu.VMEM((N, 2, D), BF16),
            pltpu.VMEM((2 * N, D), F32),
            pltpu.VMEM((N, 2, D), BF16),
            pltpu.VMEM((N, 2, D), BF16),
            pltpu.SemaphoreType.DMA((7 + PARTS,)),
            pltpu.SemaphoreType.DMA((HOPS + 2 * PARTS,)),
            pltpu.SemaphoreType.DMA((HOPS + 2 * PARTS,)),
        ],
        compiler_params=pltpu.CompilerParams(
            collective_id=0, has_side_effects=True, vmem_limit_bytes=60 << 20
        ),
    )(
        lengths,
        move_offset,
        pair_mask[None, :],
        keep_list,
        merge_index,
        merge_table[None, :],
        qk_scale,
        attn_rate,
        mlp_rate,
        up_scale,
        gate_scale,
        tokens,
        kv_cache,
        w_qkv.T,
        w_out.T,
        w_up.T,
        w_gate.T,
        w_down,
    )


def solution(mesh):
    return jax.shard_map(
        per_device,
        mesh=mesh,
        in_specs=(
            P(("group", "shard"), None),
            P(("group", "shard"), None, None),
            P(("group", "shard"), None),
            P(("group", "shard")),
            P(("group", "shard"), None),
            P(),
            P("shard", None),
            P("shard"),
            P(None, "shard"),
            P(None, "shard"),
            P(None, "shard"),
            P(None, "shard"),
            P("shard", None),
            P(),
            P(),
            P(),
            P("shard"),
            P("shard"),
        ),
        out_specs=(P(("group", "shard"), None), P(("group", "shard"), None, None)),
        check_vma=False,
    )
```

time: 91.2 us -> 75.1 us (0.82)
  local copies, waits for them, and re-layouts: 12.3 us -> 1.65 us
  Pallas kernels: 77 us -> 72 us
    unnamed x24 -> x2, local copies, waits for them, and re-layouts: 8.82 us -> 1.65 us
    pallas_call x1, Pallas kernels: 77 us -> 72 us  [per_device(): pl.pallas_call(layer_kernel, out_shape=(pltpu.VMEM((2, D), BF16), pltpu.V...]
    reshape x5 -> x0, local copies, waits for them, and re-layouts: 3.47 us -> none  [row(): return vector.reshape(1, -1)]
where the time goes in v2:
time: 75.1 us; the launch traced here: 75 us
  Pallas kernels  72 us (96%)
  local copies, waits for them, and re-layouts  1.65 us (2%)
  between operations  1.29 us (2%)
    pallas_call x1, Pallas kernels, per_device(): pl.pallas_call(layer_kernel, out_shape=(pltpu.VMEM((2, D), BF16), pltpu.V...  72 us
    unnamed x2, local copies, waits for them, and re-layouts  1.65 us

profile of v2, /device:TPU:1, one launch (start us, length us, event | category | flops | bytes accessed | tf_op | source)
XLA Modules:
  0.0 75.0 jit_solution(11536416955358536837)
XLA Ops:
  1.3 72.0 %shard_map.185 = (bf16[2,1280]{1,0:T(2,128)(2,1)S(1)}, bf16[2,128,2560]{2,1,0:T(8,128)(2,1)S(1)}) custom-call(s32[2]{0:T(128)} %lengths.1, s32[1,2]{1,0:T(1,128)} %offsets.1, s32[1,1]{1,0:T(1,128)} %bitcast.6.pair_bits, s32[2,128]{1,0:T(2,128)} %keep_ref.1, s32[2,128]{1,0:T(2,128)} %index_ref.1, bf16[1,16]{1,0:T(2,128)(2,1)} %bitcast.11, f32[1280]{0:T(1024)} %qk_ref.1, ...), custom_call_target="tpu_custom_call" | custom-call | tf_op jit(solution)/shard_map/pallas_call | solution.py:469
  73.3 0.6 copy.22
  73.9 1.1 %copy.23 = bf16[2,128,2560]{2,1,0:T(8,128)(2,1)} copy(bf16[2,128,2560]{2,1,0:T(8,128)(2,1)S(1)} %get-tuple-element.3) | data formatting | bytes 2621440

commit v3 on v2

--- a/solution.py
+++ b/solution.py
@@ -41,6 +41,26 @@
 
 
 def layer_kernel(
+    lengths_hbm,
+    offsets_hbm,
+    pair_bits_hbm,
+    keep_hbm,
+    index_hbm,
+    table_hbm,
+    qk_hbm,
+    attn_rate_hbm,
+    mlp_rate_hbm,
+    up_scale_hbm,
+    gate_scale_hbm,
+    tokens_hbm,
+    kv_hbm,
+    w_qkv_hbm,
+    w_out_hbm,
+    w_up_hbm,
+    w_gate_hbm,
+    w_down_hbm,
+    hidden_out,
+    cache_out,
     lengths,
     offsets,
     pair_bits,
@@ -52,15 +72,6 @@
     mlp_rate_ref,
     up_scale_ref,
     gate_scale_ref,
-    tokens_hbm,
-    kv_hbm,
-    w_qkv_hbm,
-    w_out_hbm,
-    w_up_hbm,
-    w_gate_hbm,
-    w_down_hbm,
-    hidden_out,
-    cache_out,
     kv,
     w_qkv,
     w_out,
@@ -99,6 +110,15 @@
     def shard_peer(k):
         return (my_group, lax.rem(my_shard + k, N))
 
+    barrier = pltpu.get_barrier_semaphore()
+
+    def greet(k, carry):
+        pl.semaphore_signal(barrier, inc=1, device_id=group_peer(k), device_id_type=MESH)
+        pl.semaphore_signal(barrier, inc=1, device_id=shard_peer(k), device_id_type=MESH)
+        return carry
+
+    lax.fori_loop(1, N, greet, 0)
+
     loads = []
     for number, (source, target) in enumerate(
         (
@@ -109,20 +129,22 @@
             (w_up_hbm, w_up),
             (w_gate_hbm, w_gate),
             (w_down_hbm, w_down),
+            (lengths_hbm, lengths),
+            (keep_hbm, keep_ref),
+            (index_hbm, index_ref),
+            (table_hbm, table_ref),
+            (offsets_hbm, offsets),
+            (pair_bits_hbm, pair_bits),
+            (qk_hbm, qk_ref),
+            (attn_rate_hbm, attn_rate_ref),
+            (mlp_rate_hbm, mlp_rate_ref),
+            (up_scale_hbm, up_scale_ref),
+            (gate_scale_hbm, gate_scale_ref),
         )
     ):
         copy = pltpu.make_async_copy(source, target, local_sem.at[number])
         copy.start()
         loads.append(copy)
-
-    barrier = pltpu.get_barrier_semaphore()
-
-    def greet(k, carry):
-        pl.semaphore_signal(barrier, inc=1, device_id=group_peer(k), device_id_type=MESH)
-        pl.semaphore_signal(barrier, inc=1, device_id=shard_peer(k), device_id_type=MESH)
-        return carry
-
-    lax.fori_loop(1, N, greet, 0)
 
     def push(source, target, peer, hop, stride=1):
         def one(k):
@@ -176,6 +198,8 @@
     def give_back(source, target, hop):
         push(lambda k: source.at[k], lambda k: target.at[k], lambda k: shard_peer(N - k), hop)
 
+    for number in range(7, 11):
+        loads[number].wait()
     rows2 = iota((2, 128), 0)
     lane = iota((1, 128), 1)
     length2 = jnp.where(rows2 == 0, lengths[0], lengths[1])
@@ -194,7 +218,7 @@
         keepdims=True,
     )
     target_row = iota((128, 128), 0).astype(F32)
-    loads[1].wait()
+    mixings = []
     for j in range(2):
         hit = iota((WTAB, 128), 0) == index_ref[j : j + 1, :]
         weights = (
@@ -203,11 +227,16 @@
         )
         placing = jnp.where(target_row == place2[j : j + 1, :], 1.0, 0.0)
         summing = jnp.where(target_row == kept[j : j + 1, :], weights, 0.0)
-        mixing = (placing + summing).astype(BF16)
-        for part in range(PARTS):
-            columns = slice(WIDE * part, WIDE * part + WIDE)
-            result = jnp.dot(mixing, kv[j, :, columns], preferred_element_type=F32)
+        mixings.append((placing + summing).astype(BF16))
+    loads[1].wait()
+
+    def compact(part):
+        columns = slice(WIDE * part, WIDE * part + WIDE)
+        for j in range(2):
+            result = jnp.dot(mixings[j], kv[j, :, columns], preferred_element_type=F32)
             packed[part, 8 * j : 8 * j + 8] = result.astype(BF16).reshape(8, 16, WIDE)
+
+    compact(0)
 
     loads[0].wait()
     pl.semaphore_wait(barrier, 2 * (N - 1))
@@ -223,8 +252,12 @@
         )
         arrived[part][0] = packed[part, my_group]
 
-    for part in range(PARTS):
+    spread_cache(0)
+    for part in range(1, PARTS):
+        compact(part)
         spread_cache(part)
+    for number in range(11, 18):
+        loads[number].wait()
 
     landing_slot = lax.div(my_group, 8)
     landing_rows = pl.ds(pl.multiple_of(16 * lax.rem(my_group, 8), 16), 16)
@@ -239,7 +272,7 @@
         push(
             lambda k: staged.at[part, k], lambda k: landing, group_peer, HOPS + PARTS + part
         )
-        own_chunk = pltpu.make_async_copy(staged.at[part, 0], landing, local_sem.at[7 + part])
+        own_chunk = pltpu.make_async_copy(staged.at[part, 0], landing, local_sem.at[18 + part])
         own_chunk.start()
         own_chunks.append(own_chunk)
 
@@ -442,6 +475,19 @@
         wait_for(ref, send_sem.at[hop])
 
 
+def finish_kernel(hidden, cache, hidden_out, cache_out, sems):
+    copies = [pltpu.make_async_copy(hidden, hidden_out, sems.at[0])]
+    for number in range(8):
+        part = (number // 4, pl.ds(32 * (number % 4), 32))
+        copies.append(
+            pltpu.make_async_copy(cache.at[part], cache_out.at[part], sems.at[1 + number])
+        )
+    for copy in copies:
+        copy.start()
+    for copy in copies:
+        copy.wait()
+
+
 def per_device(
     tokens,
     kv_cache,
@@ -462,19 +508,29 @@
     up_scale,
     gate_scale,
 ):
-    smem = pl.BlockSpec(memory_space=pltpu.SMEM)
     vmem = pl.BlockSpec(memory_space=pltpu.VMEM)
     hbm = pl.BlockSpec(memory_space=pltpu.HBM)
 
-    return pl.pallas_call(
+    hidden, cache = pl.pallas_call(
         layer_kernel,
         out_shape=(
             pltpu.VMEM((2, D), BF16),
             pltpu.VMEM((2, 128, 2 * D), BF16),
         ),
-        in_specs=[smem] * 3 + [vmem] * 8 + [hbm] * 7,
+        in_specs=[hbm] * 18,
         out_specs=(vmem, pl.BlockSpec(memory_space=pl.ANY)),
         scratch_shapes=[
+            pltpu.SMEM((2,), jnp.int32),
+            pltpu.SMEM((1, 2), jnp.int32),
+            pltpu.SMEM((1, 1), jnp.int32),
+            pltpu.VMEM((2, 128), jnp.int32),
+            pltpu.VMEM((2, 128), jnp.int32),
+            pltpu.VMEM((1, WTAB), BF16),
+            pltpu.VMEM((D,), F32),
+            pltpu.VMEM((D,), F32),
+            pltpu.VMEM((D,), F32),
+            pltpu.VMEM((320,), F32),
+            pltpu.VMEM((320,), F32),
             pltpu.VMEM((2, 128, 2 * D), BF16),
             pltpu.VMEM((240, D), BF16),
             pltpu.VMEM((80, D), BF16),
@@ -500,7 +556,7 @@
             pltpu.VMEM((2 * N, D), F32),
             pltpu.VMEM((N, 2, D), BF16),
             pltpu.VMEM((N, 2, D), BF16),
-            pltpu.SemaphoreType.DMA((7 + PARTS,)),
+            pltpu.SemaphoreType.DMA((18 + PARTS,)),
             pltpu.SemaphoreType.DMA((HOPS + 2 * PARTS,)),
             pltpu.SemaphoreType.DMA((HOPS + 2 * PARTS,)),
         ],
@@ -526,6 +582,19 @@
         w_up.T,
         w_gate.T,
         w_down,
+    )
+    return pl.pallas_call(
+        finish_kernel,
+        out_shape=(
+            pltpu.HBM((2, D), BF16),
+            pltpu.HBM((2, 128, 2 * D), BF16),
+        ),
+        in_specs=[pl.BlockSpec(memory_space=pl.ANY)] * 2,
+        out_specs=(pl.BlockSpec(memory_space=pl.ANY),) * 2,
+        scratch_shapes=[pltpu.SemaphoreType.DMA((9,))],
+    )(
+        pltpu.with_memory_space_constraint(hidden, pltpu.VMEM),
+        pltpu.with_memory_space_constraint(cache, pltpu.VMEM),
     )
 
 

time: 75.1 us -> 73.8 us (0.983)
  local copies, waits for them, and re-layouts: 1.65 us -> 0 us
    unnamed x2 -> x0, local copies, waits for them, and re-layouts: 1.65 us -> none
    pallas_call x0 -> x1, Pallas kernels: none -> 1.13 us  [per_device(): pl.pallas_call(finish_kernel, out_shape=(pltpu.HBM((2, D), BF16), pltpu.H...]
where the time goes in v3:
time: 73.8 us; the launch traced here: 73.7 us
  Pallas kernels  72.4 us (98%)
  between operations  1.29 us (2%)
    pallas_call x1, Pallas kernels, per_device(): pl.pallas_call(layer_kernel, out_shape=(pltpu.VMEM((2, D), BF16), pltpu.V...  71.3 us

profile of v3, /device:TPU:1, one launch (start us, length us, event | category | flops | bytes accessed | tf_op | source)
XLA Modules:
  0.0 73.7 jit_solution(4752850331696752168)
XLA Ops:
  1.3 71.3 %shard_map.185 = (bf16[2,1280]{1,0:T(2,128)(2,1)S(1)}, bf16[2,128,2560]{2,1,0:T(8,128)(2,1)S(1)}) custom-call(s32[2]{0:T(128)} %lengths_hbm.1, s32[1,2]{1,0:T(1,128)} %offsets_hbm.1, s32[1,1]{1,0:T(1,128)} %bitcast.6.pair_bits_hbm, s32[2,128]{1,0:T(2,128)} %keep_hbm.1, s32[2,128]{1,0:T(2,128)} %index_hbm.1, bf16[1,16]{1,0:T(2,128)(2,1)} %bitcast.11, ...), custom_call_target="tpu_custom_call" | custom-call | tf_op jit(solution)/shard_map/pallas_call | solution.py:514
  72.6 1.1 %shard_map.186 = (bf16[2,1280]{1,0:T(2,128)(2,1)}, bf16[2,128,2560]{2,1,0:T(8,128)(2,1)}) custom-call(bf16[2,1280]{1,0:T(2,128)(2,1)S(1)} %get-tuple-element.4.hidden, bf16[2,128,2560]{2,1,0:T(8,128)(2,1)S(1)} %get-tuple-element.5.cache), custom_call_target="tpu_custom_call" | custom-call | tf_op jit(solution)/shard_map/pallas_call | solution.py:586

commit v4 on v3

--- a/solution.py
+++ b/solution.py
@@ -269,9 +269,20 @@
         for m in range(N):
             staged[part, m] = arrived[part][lax.rem(my_offset + N - m, N)]
         landing = cache_out.at[landing_slot, landing_rows, pl.ds(WIDE * part, WIDE)]
-        push(
-            lambda k: staged.at[part, k], lambda k: landing, group_peer, HOPS + PARTS + part
-        )
+        def one(target, carry):
+            @pl.when(target != my_group)
+            def _():
+                pltpu.make_async_remote_copy(
+                    src_ref=staged.at[part, lax.rem(target - my_group + N, N)],
+                    dst_ref=landing,
+                    send_sem=send_sem.at[HOPS + PARTS + part],
+                    recv_sem=recv_sem.at[HOPS + PARTS + part],
+                    device_id=(target, my_shard),
+                    device_id_type=MESH,
+                ).start()
+            return carry
+
+        lax.fori_loop(0, N, one, 0)
         own_chunk = pltpu.make_async_copy(staged.at[part, 0], landing, local_sem.at[18 + part])
         own_chunk.start()
         own_chunks.append(own_chunk)

time: 73.8 us -> 72.3 us (0.980)
  Pallas kernels: 72.4 us -> 70.7 us
    pallas_call x1, Pallas kernels: 71.3 us -> 69.5 us  [per_device(): pl.pallas_call(layer_kernel, out_shape=(pltpu.VMEM((2, D), BF16), pltpu.V...]
where the time goes in v4:
time: 72.3 us; the launch traced here: 72 us
  Pallas kernels  70.7 us (98%)
  between operations  1.29 us (2%)
    pallas_call x1, Pallas kernels, per_device(): pl.pallas_call(layer_kernel, out_shape=(pltpu.VMEM((2, D), BF16), pltpu.V...  69.5 us

profile of v4, /device:TPU:1, one launch (start us, length us, event | category | flops | bytes accessed | tf_op | source)
XLA Modules:
  0.0 72.0 jit_solution(14612995836564817350)
XLA Ops:
  1.3 69.5 %shard_map.185 = (bf16[2,1280]{1,0:T(2,128)(2,1)S(1)}, bf16[2,128,2560]{2,1,0:T(8,128)(2,1)S(1)}) custom-call(s32[2]{0:T(128)} %lengths_hbm.1, s32[1,2]{1,0:T(1,128)} %offsets_hbm.1, s32[1,1]{1,0:T(1,128)} %bitcast.6.pair_bits_hbm, s32[2,128]{1,0:T(2,128)} %keep_hbm.1, s32[2,128]{1,0:T(2,128)} %index_hbm.1, bf16[1,16]{1,0:T(2,128)(2,1)} %bitcast.11, ...), custom_call_target="tpu_custom_call" | custom-call | tf_op jit(solution)/shard_map/pallas_call | solution.py:525
  70.8 1.1 %shard_map.186 = (bf16[2,1280]{1,0:T(2,128)(2,1)}, bf16[2,128,2560]{2,1,0:T(8,128)(2,1)}) custom-call(bf16[2,1280]{1,0:T(2,128)(2,1)S(1)} %get-tuple-element.4.hidden, bf16[2,128,2560]{2,1,0:T(8,128)(2,1)S(1)} %get-tuple-element.5.cache), custom_call_target="tpu_custom_call" | custom-call | tf_op jit(solution)/shard_map/pallas_call | solution.py:597

commit v5 on v4

--- a/solution.py
+++ b/solution.py
@@ -12,9 +12,10 @@
 WTAB = 16
 N = 16
 D = 1280
-PARTS = 2
+PARTS = 4
 WIDE = 2 * D // PARTS
 KEY_PARTS = PARTS // 2
+PIECES = D // 128
 HOPS = 10
 HEADS_PAD = 32
 EPSILON = 1e-06
@@ -81,7 +82,11 @@
     packed,
     arrived,
     staged,
-    group_rows,
+    own_rows,
+    piece_send,
+    piece_recv,
+    turn_send,
+    turn_recv,
     shard_rows,
     lhs,
     qkv_send,
@@ -122,8 +127,8 @@
     loads = []
     for number, (source, target) in enumerate(
         (
-            (tokens_hbm, group_rows.at[0]),
-            (kv_hbm, kv),
+            (tokens_hbm, own_rows),
+            (kv_hbm.at[:, :, pl.ds(0, WIDE)], kv.at[:, :, pl.ds(0, WIDE)]),
             (w_qkv_hbm, w_qkv),
             (w_out_hbm, w_out),
             (w_up_hbm, w_up),
@@ -145,6 +150,12 @@
         copy = pltpu.make_async_copy(source, target, local_sem.at[number])
         copy.start()
         loads.append(copy)
+    rest_of_kv = pltpu.make_async_copy(
+        kv_hbm.at[:, :, pl.ds(WIDE, 2 * D - WIDE)],
+        kv.at[:, :, pl.ds(WIDE, 2 * D - WIDE)],
+        local_sem.at[18 + PARTS],
+    )
+    rest_of_kv.start()
 
     def push(source, target, peer, hop, stride=1):
         def one(k):
@@ -239,9 +250,23 @@
     compact(0)
 
     loads[0].wait()
+    for piece in range(PIECES):
+        columns = slice(128 * piece, 128 * piece + 128)
+        piece_send[(piece + PIECES // 2) % PIECES] = own_rows[:, columns]
+        if piece == PIECES // 2:
+            piece_recv[0] = own_rows[:, columns]
     pl.semaphore_wait(barrier, 2 * (N - 1))
 
-    gather_group(group_rows, 0)
+    for slot in range(1, PIECES):
+        distance = slot if slot < PIECES // 2 else slot - PIECES
+        pltpu.make_async_remote_copy(
+            src_ref=piece_send.at[slot],
+            dst_ref=piece_recv.at[slot],
+            send_sem=send_sem.at[0],
+            recv_sem=recv_sem.at[0],
+            device_id=group_peer(distance + N),
+            device_id_type=MESH,
+        ).start()
 
     def spread_cache(part):
         push(
@@ -253,11 +278,29 @@
         arrived[part][0] = packed[part, my_group]
 
     spread_cache(0)
+    rest_of_kv.wait()
     for part in range(1, PARTS):
         compact(part)
-        spread_cache(part)
     for number in range(11, 18):
         loads[number].wait()
+
+    offset0 = offsets[0, 0]
+    offset1 = offsets[0, 1]
+    narrow = iota((2, 128), 0) == 0
+    wait_for(piece_recv.at[pl.ds(1, PIECES - 1)], recv_sem.at[0])
+
+    def piece_for(m, offset):
+        piece = lax.rem(PIECES // 2 - m - offset + 2 * N, N)
+        slot = lax.rem(jnp.minimum(piece, PIECES - 1) + PIECES // 2, PIECES)
+        return piece_recv[slot].astype(F32)
+
+    for m in range(N):
+        turned = jnp.where(narrow, piece_for(m, offset0), piece_for(m, offset1))
+        turn_send[m] = turned.astype(BF16)
+    turn_recv[0] = turn_send[0]
+    push(lambda k: turn_send.at[k], lambda k: turn_recv.at[k], group_peer, 8)
+    spread_cache(1)
+    spread_cache(2)
 
     landing_slot = lax.div(my_group, 8)
     landing_rows = pl.ds(pl.multiple_of(16 * lax.rem(my_group, 8), 16), 16)
@@ -266,14 +309,15 @@
 
     def deliver_cache(part):
         wait_for(others(arrived[part]), recv_sem.at[HOPS + part])
-        for m in range(N):
-            staged[part, m] = arrived[part][lax.rem(my_offset + N - m, N)]
         landing = cache_out.at[landing_slot, landing_rows, pl.ds(WIDE * part, WIDE)]
         def one(target, carry):
+            m = lax.rem(target - my_group + N, N)
+            staged[part, m] = arrived[part][lax.rem(my_offset + N - m, N)]
+
             @pl.when(target != my_group)
             def _():
                 pltpu.make_async_remote_copy(
-                    src_ref=staged.at[part, lax.rem(target - my_group + N, N)],
+                    src_ref=staged.at[part, m],
                     dst_ref=landing,
                     send_sem=send_sem.at[HOPS + PARTS + part],
                     recv_sem=recv_sem.at[HOPS + PARTS + part],
@@ -287,17 +331,17 @@
         own_chunk.start()
         own_chunks.append(own_chunk)
 
-    relay_group(group_rows, 0, 8)
-    offset0 = offsets[0, 0]
-    offset1 = offsets[0, 1]
     first = iota((2, D), 0) == 0
-    own_tokens = group_rows[0].astype(F32)
-    moved_tokens = jnp.where(
-        first,
-        group_rows[slot_of(my_group + offset0)].astype(F32),
-        group_rows[slot_of(my_group + offset1)].astype(F32),
-    )
-    shard_rows[0] = moved_tokens.astype(BF16)
+    own_tokens = own_rows[...].astype(F32)
+    wait_for(others(turn_recv), recv_sem.at[8])
+    for piece in range(PIECES):
+        back = PIECES // 2 - piece + 2 * N
+        moved = jnp.where(
+            narrow,
+            turn_recv[lax.rem(back - offset0, N)].astype(F32),
+            turn_recv[lax.rem(back - offset1, N)].astype(F32),
+        )
+        shard_rows[0, :, 128 * piece : 128 * piece + 128] = moved.astype(BF16)
     gather(shard_rows, shard_peer, 1)
 
     def stack(rows):
@@ -326,6 +370,7 @@
 
     loads[2].wait()
     wait_for(others(shard_rows), recv_sem.at[1])
+    spread_cache(3)
     spread_back(stack(shard_rows), w_qkv[...], 240, 384, qkv_send, qkv_recv, qkv_flat, 2)
 
     head_mask = lax.shift_right_logical(iota((HEADS_PAD, D), 1), 6) == iota((HEADS_PAD, D), 0)
@@ -396,7 +441,8 @@
 
     gather_group(partial, 3)
 
-    deliver_cache(0)
+    for part in range(3):
+        deliver_cache(part)
 
     relay_group(partial, 3, 9)
     partner = jnp.bitwise_xor(my_group, pair_bits[0, 0])
@@ -425,8 +471,7 @@
     )
     attended_rows[0] = attended.astype(BF16)
     gather(attended_rows, shard_peer, 4)
-    for part in range(1, PARTS):
-        deliver_cache(part)
+    deliver_cache(3)
 
     loads[3].wait()
     wait_for(others(attended_rows), recv_sem.at[4])
@@ -468,7 +513,7 @@
     most = pl.ds(1, N // 2 - 1)
     sent = (
         [
-            group_rows.at[most],
+            piece_recv.at[pl.ds(1, PIECES - 1)],
             others(shard_rows),
             others(qkv_recv),
             partial.at[most],
@@ -476,7 +521,7 @@
             others(out_recv),
             others(mixed_rows),
             others(sum_recv),
-            group_rows.at[half],
+            others(turn_recv),
             partial.at[half],
         ]
         + [others(arrived[part]) for part in range(PARTS)]
@@ -551,7 +596,11 @@
             pltpu.VMEM((PARTS, N, 16, WIDE), BF16),
             [pltpu.VMEM((N, 16, WIDE), BF16)] * PARTS,
             pltpu.VMEM((PARTS, N, 16, WIDE), BF16),
-            pltpu.VMEM((N, 2, D), BF16),
+            pltpu.VMEM((2, D), BF16),
+            pltpu.VMEM((PIECES, 2, 128), BF16),
+            pltpu.VMEM((PIECES, 2, 128), BF16),
+            pltpu.VMEM((N, 2, 128), BF16),
+            pltpu.VMEM((N, 2, 128), BF16),
             pltpu.VMEM((N, 2, D), BF16),
             pltpu.VMEM((2 * N, D), F32),
             pltpu.VMEM((N, 2, 384), F32),
@@ -567,7 +616,7 @@
             pltpu.VMEM((2 * N, D), F32),
             pltpu.VMEM((N, 2, D), BF16),
             pltpu.VMEM((N, 2, D), BF16),
-            pltpu.SemaphoreType.DMA((18 + PARTS,)),
+            pltpu.SemaphoreType.DMA((19 + PARTS,)),
             pltpu.SemaphoreType.DMA((HOPS + 2 * PARTS,)),
             pltpu.SemaphoreType.DMA((HOPS + 2 * PARTS,)),
         ],

time: 72.3 us -> 71.8 us (level)
  no operation moved by 1% of the time
where the time goes in v5:
time: 71.8 us; the launch traced here: 71.7 us
  Pallas kernels  70.4 us (98%)
  between operations  1.29 us (2%)
    pallas_call x1, Pallas kernels, per_device(): pl.pallas_call(layer_kernel, out_shape=(pltpu.VMEM((2, D), BF16), pltpu.V...  69.2 us

profile of v5, /device:TPU:1, one launch (start us, length us, event | category | flops | bytes accessed | tf_op | source)
XLA Modules:
  0.0 71.7 jit_solution(10029731235702737323)
XLA Ops:
  1.3 69.2 %shard_map.185 = (bf16[2,1280]{1,0:T(2,128)(2,1)S(1)}, bf16[2,128,2560]{2,1,0:T(8,128)(2,1)S(1)}) custom-call(s32[2]{0:T(128)} %lengths_hbm.1, s32[1,2]{1,0:T(1,128)} %offsets_hbm.1, s32[1,1]{1,0:T(1,128)} %bitcast.6.pair_bits_hbm, s32[2,128]{1,0:T(2,128)} %keep_hbm.1, s32[2,128]{1,0:T(2,128)} %index_hbm.1, bf16[1,16]{1,0:T(2,128)(2,1)} %bitcast.11, ...), custom_call_target="tpu_custom_call" | custom-call | tf_op jit(solution)/shard_map/pallas_call | solution.py:570
  70.5 1.1 %shard_map.186 = (bf16[2,1280]{1,0:T(2,128)(2,1)}, bf16[2,128,2560]{2,1,0:T(8,128)(2,1)}) custom-call(bf16[2,1280]{1,0:T(2,128)(2,1)S(1)} %get-tuple-element.4.hidden, bf16[2,128,2560]{2,1,0:T(8,128)(2,1)S(1)} %get-tuple-element.5.cache), custom_call_target="tpu_custom_call" | custom-call | tf_op jit(solution)/shard_map/pallas_call | solution.py:646

commit v6 on v5

--- a/solution.py
+++ b/solution.py
@@ -148,14 +148,17 @@
         )
     ):
         copy = pltpu.make_async_copy(source, target, local_sem.at[number])
-        copy.start()
         loads.append(copy)
+    for number in (7, 8, 9, 10, 0, 1):
+        loads[number].start()
     rest_of_kv = pltpu.make_async_copy(
         kv_hbm.at[:, :, pl.ds(WIDE, 2 * D - WIDE)],
         kv.at[:, :, pl.ds(WIDE, 2 * D - WIDE)],
         local_sem.at[18 + PARTS],
     )
     rest_of_kv.start()
+    for number in (11, 12, 13, 14, 15, 16, 17, 2, 3, 4, 5, 6):
+        loads[number].start()
 
     def push(source, target, peer, hop, stride=1):
         def one(k):

time: 71.8 us -> 71.8 us (level)
  no operation moved by 1% of the time
where the time goes in v6:
time: 71.8 us; the launch traced here: 71.7 us
  Pallas kernels  70.4 us (98%)
  between operations  1.29 us (2%)
    pallas_call x1, Pallas kernels, per_device(): pl.pallas_call(layer_kernel, out_shape=(pltpu.VMEM((2, D), BF16), pltpu.V...  69.2 us

profile of v6, /device:TPU:1, one launch (start us, length us, event | category | flops | bytes accessed | tf_op | source)
XLA Modules:
  0.0 71.7 jit_solution(7576095204536219242)
XLA Ops:
  1.3 69.2 %shard_map.185 = (bf16[2,1280]{1,0:T(2,128)(2,1)S(1)}, bf16[2,128,2560]{2,1,0:T(8,128)(2,1)S(1)}) custom-call(s32[2]{0:T(128)} %lengths_hbm.1, s32[1,2]{1,0:T(1,128)} %offsets_hbm.1, s32[1,1]{1,0:T(1,128)} %bitcast.6.pair_bits_hbm, s32[2,128]{1,0:T(2,128)} %keep_hbm.1, s32[2,128]{1,0:T(2,128)} %index_hbm.1, bf16[1,16]{1,0:T(2,128)(2,1)} %bitcast.11, ...), custom_call_target="tpu_custom_call" | custom-call | tf_op jit(solution)/shard_map/pallas_call | solution.py:573
  70.5 1.1 %shard_map.186 = (bf16[2,1280]{1,0:T(2,128)(2,1)}, bf16[2,128,2560]{2,1,0:T(8,128)(2,1)}) custom-call(bf16[2,1280]{1,0:T(2,128)(2,1)S(1)} %get-tuple-element.4.hidden, bf16[2,128,2560]{2,1,0:T(8,128)(2,1)S(1)} %get-tuple-element.5.cache), custom_call_target="tpu_custom_call" | custom-call | tf_op jit(solution)/shard_map/pallas_call | solution.py:649
